TPU v7x, 32 devices: a whole 2x2x4 slice. The times are simulated.
32 devices in a mesh: dp: 4 (over y, core), ulysses: 2 (over x), blk: 4 (over z).
Axes of the slice: x: 2, y: 2, z: 4, core: 2. Of those that a mesh axis runs over, the one named last changes fastest.
Arguments:
- tokens: bfloat16 [2, 2048, 2560], P(None, ('dp', 'ulysses', 'blk')), may hold values from -6 to 6
- segments: int32 [2, 2048], P(None, ('dp', 'ulysses', 'blk')), may hold values from 0 to 3, never falling along the last dimension, each value on 1 to 2000 neighbouring positions
- norm1: bfloat16 [2560], P(('dp', 'ulysses', 'blk')), may hold values from 0.099609375 to 1.8984375
- wq: bfloat16 [2560, 2560], P(('dp', 'ulysses'), 'blk'), may hold values from -0.125 to 0.125
- wk: bfloat16 [2560, 640], P(('dp', 'ulysses'), 'blk'), may hold values from -0.125 to 0.125
- wv: bfloat16 [2560, 640], P(('dp', 'ulysses'), 'blk'), may hold values from -0.125 to 0.125
- wo: bfloat16 [2560, 2560], P(('dp', 'ulysses'), 'blk'), may hold values from -1 to 1
- norm2: bfloat16 [2560], P(('dp', 'ulysses', 'blk')), may hold values from 0.099609375 to 1.8984375
- w_gate: bfloat16 [2560, 7168], P(('dp', 'ulysses'), 'blk'), may hold values from -0.125 to 0.125
- w_up: bfloat16 [2560, 7168], P(('dp', 'ulysses'), 'blk'), may hold values from -0.125 to 0.125
- w_down: bfloat16 [7168, 2560], P(('dp', 'ulysses'), 'blk'), may hold values from -0.0625 to 0.0625
- cotangent: bfloat16 [2, 2048, 2560], P(None, ('dp', 'ulysses', 'blk')), may hold values from -6 to 6
Outputs:
- out: bfloat16 [2, 2048, 2560], P(None, ('dp', 'ulysses', 'blk'))
- d_input: float32 [2, 2048, 2560], P(None, ('dp', 'ulysses', 'blk'))
- grad_norm1: float32 [2560], P(('dp', 'ulysses', 'blk'))
- grad_wq: float32 [2560, 2560], P(('dp', 'ulysses'), 'blk')
- grad_wk: float32 [2560, 640], P(('dp', 'ulysses'), 'blk')
- grad_wv: float32 [2560, 640], P(('dp', 'ulysses'), 'blk')
- grad_wo: float32 [2560, 2560], P(('dp', 'ulysses'), 'blk')
- grad_norm2: float32 [2560], P(('dp', 'ulysses', 'blk'))
- grad_gate: float32 [2560, 7168], P(('dp', 'ulysses'), 'blk')
- grad_up: float32 [2560, 7168], P(('dp', 'ulysses'), 'blk')
- grad_down: float32 [7168, 2560], P(('dp', 'ulysses'), 'blk')
Inputs may be any that keep to these rules, and one draw needn't show every extreme that they name: `segments`: along each row the numbers never fall; each of 0 to 3 takes one run of 1 to 2000 consecutive tokens, and one run has exactly 2000.
All inputs are finite; a program needn't handle non-finite values.
Results may differ from a plain program's by a relative error of at most 0.025.
Values may be sent and summed in bfloat16 or wider, within the bound.
No kernel may reach another device: no remote copies, remote signals or barrier semaphores. Data moves between devices by JAX's collectives and lax.ppermute only.
A program may use at most 832 MiB of HBM per device.

v0:
```python
import math

import jax
import jax.numpy as jnp
from jax import lax
from jax.sharding import PartitionSpec as P

HD = 80


epsilon = 1e-05
rope_base = 1000000.0
masked_score = -1e30
key_width = 512
gain_block = 128


def inverse_norm(values):
    return lax.rsqrt(jnp.mean(values * values, axis=-1, keepdims=True) + epsilon)


def norm_back(grad_normed, gain_full, unit_rows, inverse):
    scaled = grad_normed * gain_full
    return inverse * (scaled - unit_rows * jnp.mean(scaled * unit_rows, axis=-1, keepdims=True))


def rotate(field, positions, direction):
    half_width = field.shape[-1] // 2
    inverse_freq = rope_base ** (-2.0 * jnp.arange(half_width, dtype=jnp.float32) / field.shape[-1])
    angles = positions.astype(jnp.float32)[:, None] * inverse_freq[None, :]
    cosine = jnp.cos(angles)[:, None, :]
    sine_part = direction * jnp.sin(angles)[:, None, :]
    first_half = field[..., :half_width]
    second = field[..., half_width:]
    return jnp.concatenate(
        [first_half * cosine - second * sine_part, second * cosine + first_half * sine_part],
        axis=-1,
    )


def gather_layer(norm1, wq, wk, wv, wo, norm2, w_gate, w_up, w_down):
    gain_a, query_w, key_w, value_w, out_w, gain_b, gate_w, up_w, down_w = (
        lax.all_gather(norm1, "blk", axis=0, tiled=True),
        lax.all_gather(wq, "blk", axis=1, tiled=True),
        lax.all_gather(wk, "blk", axis=1, tiled=True),
        lax.all_gather(wv, "blk", axis=1, tiled=True),
        lax.all_gather(wo, "blk", axis=1, tiled=True),
        lax.all_gather(norm2, "blk", axis=0, tiled=True),
        lax.all_gather(w_gate, "blk", axis=1, tiled=True),
        lax.all_gather(w_up, "blk", axis=1, tiled=True),
        lax.all_gather(w_down, "blk", axis=1, tiled=True),
    )
    return (
        lax.all_gather(gain_a, ("dp", "ulysses"), axis=0, tiled=True),
        lax.all_gather(query_w, ("dp", "ulysses"), axis=0, tiled=True),
        lax.all_gather(key_w, ("dp", "ulysses"), axis=0, tiled=True),
        lax.all_gather(value_w, ("dp", "ulysses"), axis=0, tiled=True),
        lax.all_gather(out_w, ("dp", "ulysses"), axis=0, tiled=True),
        lax.all_gather(gain_b, ("dp", "ulysses"), axis=0, tiled=True),
        lax.all_gather(gate_w, ("dp", "ulysses"), axis=0, tiled=True),
        lax.all_gather(up_w, ("dp", "ulysses"), axis=0, tiled=True),
        lax.all_gather(down_w, ("dp", "ulysses"), axis=0, tiled=True),
    )


def query_layout(seq_seg, tok_rows, part_count):
    part_len = seq_seg.shape[0] // part_count
    offset = lax.axis_index("blk") * tok_rows
    local_index = jnp.arange(tok_rows, dtype=jnp.int32)
    query_index = (
        jnp.arange(part_count, dtype=jnp.int32)[:, None] * part_len + offset + local_index[None, :]
    )
    query_seg = lax.dynamic_slice_in_dim(seq_seg.reshape(part_count, part_len), offset, tok_rows, 1)
    return (query_index, query_seg)


def visibility(seq_seg, query_index, query_seg, block_start, key_count):
    key_index = block_start + jnp.arange(key_count, dtype=jnp.int32)
    key_seg = lax.dynamic_slice_in_dim(seq_seg, block_start, key_count)
    return (key_seg[None, :] == query_seg[:, None]) & (key_index[None, :] <= query_index[:, None])


def keep_state(stats_in):
    return stats_in


def forward_block(query_part, key_block, value_block, visible, score_scale):

    def update(stats_in):
        running_max, running_sum, running_acc = stats_in
        scores = (
            jnp.einsum("qkgd,jkd->kgqj", query_part, key_block, preferred_element_type=jnp.float32)
            * score_scale
        )
        scores = jnp.where(visible[None, None], scores, masked_score)
        new_max = jnp.maximum(running_max, jnp.max(scores, axis=-1))
        weights = jnp.where(visible[None, None], jnp.exp(scores - new_max[..., None]), 0.0)
        shrink = jnp.exp(running_max - new_max)
        new_sum = running_sum * shrink + jnp.sum(weights, axis=-1)
        new_acc = running_acc * shrink[..., None] + jnp.einsum(
            "kgqj,jkd->kgqd",
            weights.astype(jnp.bfloat16),
            value_block,
            preferred_element_type=jnp.float32,
        )
        return (new_max, new_sum, new_acc)

    return update


def backward_block(
    query_part, grad_part, key_block, value_block, visible, log_sum, delta, score_scale
):

    def update(grads_in):
        grad_query, grad_key, grad_value = grads_in
        scores = (
            jnp.einsum("qkgd,jkd->kgqj", query_part, key_block, preferred_element_type=jnp.float32)
            * score_scale
        )
        probabilities = jnp.where(visible[None, None], jnp.exp(scores - log_sum[..., None]), 0.0)
        grad_value = grad_value + jnp.einsum(
            "kgqj,qkgd->jkd",
            probabilities.astype(jnp.bfloat16),
            grad_part,
            preferred_element_type=jnp.float32,
        )
        grad_probs = jnp.einsum(
            "qkgd,jkd->kgqj", grad_part, value_block, preferred_element_type=jnp.float32
        )
        grad_scores = (probabilities * (grad_probs - delta[..., None])).astype(jnp.bfloat16)
        grad_query = grad_query + score_scale * jnp.einsum(
            "kgqj,jkd->kgqd", grad_scores, key_block, preferred_element_type=jnp.float32
        )
        grad_key = grad_key + score_scale * jnp.einsum(
            "kgqj,qkgd->jkd", grad_scores, query_part, preferred_element_type=jnp.float32
        )
        return (grad_query, grad_key, grad_value)

    return update


def attend_forward(queries, keys, values, seq_seg, query_index, query_seg):
    part_count, tok_rows, kv_local, group_size, head_dim = queries.shape
    seq_len = keys.shape[0]
    key_count = math.gcd(key_width, seq_len // part_count)
    score_scale = head_dim ** (-0.5)

    def scan_step(running, block_index):
        block_start = block_index * key_count
        key_block = lax.dynamic_slice_in_dim(keys, block_start, key_count, 0)
        value_block = lax.dynamic_slice_in_dim(values, block_start, key_count, 0)
        updated = []
        for part_index in range(part_count):
            visible = visibility(
                seq_seg, query_index[part_index], query_seg[part_index], block_start, key_count
            )
            update = forward_block(
                queries[part_index], key_block, value_block, visible, score_scale
            )
            updated.append(lax.cond(jnp.any(visible), update, keep_state, running[part_index]))
        return (tuple(updated), None)

    initial = tuple(
        (
            (
                jnp.full((kv_local, group_size, tok_rows), masked_score, jnp.float32),
                jnp.zeros((kv_local, group_size, tok_rows), jnp.float32),
                jnp.zeros((kv_local, group_size, tok_rows, head_dim), jnp.float32),
            )
            for part_index in range(part_count)
        )
    )
    finished, unused = lax.scan(
        scan_step, initial, jnp.arange(seq_len // key_count, dtype=jnp.int32)
    )
    outputs = jnp.stack([part_stats[2] / part_stats[1][..., None] for part_stats in finished])
    log_sums = jnp.stack([part_stats[0] + jnp.log(part_stats[1]) for part_stats in finished])
    return (outputs, log_sums)


def attend_backward(
    queries, keys, values, seq_seg, query_index, query_seg, grad_out, outputs, log_sums
):
    part_count, tok_rows, kv_local, group_size, head_dim = queries.shape
    seq_len = keys.shape[0]
    key_count = math.gcd(key_width, seq_len // part_count)
    score_scale = head_dim ** (-0.5)
    delta_all = jnp.einsum("pqkgd,pkgqd->pkgq", grad_out.astype(jnp.float32), outputs)

    def scan_step(running, block_index):
        block_start = block_index * key_count
        key_block = lax.dynamic_slice_in_dim(keys, block_start, key_count, 0)
        value_block = lax.dynamic_slice_in_dim(values, block_start, key_count, 0)
        grad_key = jnp.zeros((key_count, kv_local, head_dim), jnp.float32)
        grad_value = jnp.zeros((key_count, kv_local, head_dim), jnp.float32)
        updated = []
        for part_index in range(part_count):
            visible = visibility(
                seq_seg, query_index[part_index], query_seg[part_index], block_start, key_count
            )
            update = backward_block(
                queries[part_index],
                grad_out[part_index],
                key_block,
                value_block,
                visible,
                log_sums[part_index],
                delta_all[part_index],
                score_scale,
            )
            grad_query, grad_key, grad_value = lax.cond(
                jnp.any(visible), update, keep_state, (running[part_index], grad_key, grad_value)
            )
            updated.append(grad_query)
        block_grads = jnp.concatenate(
            [
                grad_key.reshape(key_count, kv_local * head_dim),
                grad_value.reshape(key_count, kv_local * head_dim),
            ],
            axis=1,
        )
        return (tuple(updated), block_grads)

    initial = tuple(
        (
            jnp.zeros((kv_local, group_size, tok_rows, head_dim), jnp.float32)
            for part_index in range(part_count)
        )
    )
    finished, key_terms = lax.scan(
        scan_step, initial, jnp.arange(seq_len // key_count, dtype=jnp.int32)
    )
    return (
        jnp.stack(finished),
        key_terms.reshape(part_count, seq_len // part_count, 2 * kv_local * head_dim),
    )


def forward_batch(tokens, own_seg, seq_seg, attn_weights, ffn_weights):
    gain1, weight_q, weight_k, weight_v, weight_o = attn_weights
    gain2, weight_gate, weight_up, weight_down = ffn_weights
    tok_rows = tokens.shape[0]
    part_count = lax.axis_size("ulysses")
    head_count = weight_q.shape[1] // HD
    kv_count = weight_k.shape[1] // HD
    group_q = weight_q.shape[1] // part_count
    group_kv = weight_k.shape[1] // part_count
    seq_len = seq_seg.shape[0]
    block_id = lax.axis_index("ulysses") * lax.axis_size("blk") + lax.axis_index("blk")
    token_index = block_id * tok_rows + jnp.arange(tok_rows, dtype=jnp.int32)
    positions = token_index - jnp.sum(
        (seq_seg[None, :] < own_seg[:, None]).astype(jnp.int32), axis=1
    )
    floats = tokens.astype(jnp.float32)
    inverse1 = inverse_norm(floats)
    unit1 = floats * inverse1
    normed1 = (unit1 * gain1.astype(jnp.float32)).astype(jnp.bfloat16)
    query_raw = jnp.dot(normed1, weight_q, preferred_element_type=jnp.float32)
    key_raw = jnp.dot(normed1, weight_k, preferred_element_type=jnp.float32)
    value_raw = jnp.dot(normed1, weight_v, preferred_element_type=jnp.float32)
    query_rot = rotate(query_raw.reshape(tok_rows, head_count, HD), positions, 1.0).astype(
        jnp.bfloat16
    )
    key_rot = rotate(key_raw.reshape(tok_rows, kv_count, HD), positions, 1.0).astype(jnp.bfloat16)
    packed = jnp.concatenate(
        [
            query_rot.reshape(tok_rows, part_count, group_q),
            key_rot.reshape(tok_rows, part_count, group_kv),
            value_raw.astype(jnp.bfloat16).reshape(tok_rows, part_count, group_kv),
        ],
        axis=2,
    )
    arrived = lax.all_to_all(packed, "ulysses", split_axis=1, concat_axis=0, tiled=True)
    queries = arrived[:, 0, :group_q].reshape(
        part_count, tok_rows, kv_count // part_count, head_count // kv_count, HD
    )
    local_kv = arrived[:, 0, group_q:].reshape(part_count, tok_rows, 2 * group_kv)
    all_kv = lax.all_gather(local_kv, "blk", axis=1, tiled=True).reshape(seq_len, 2 * group_kv)
    keys = all_kv[:, :group_kv].reshape(seq_len, kv_count // part_count, HD)
    values = all_kv[:, group_kv:].reshape(seq_len, kv_count // part_count, HD)
    query_index, query_seg = query_layout(seq_seg, tok_rows, part_count)
    outputs, log_sums = attend_forward(queries, keys, values, seq_seg, query_index, query_seg)
    sending = (
        outputs.transpose(0, 3, 1, 2, 4)
        .reshape(part_count, tok_rows, 1, group_q)
        .astype(jnp.bfloat16)
    )
    attended = lax.all_to_all(sending, "ulysses", split_axis=0, concat_axis=2, tiled=True).reshape(
        tok_rows, part_count * group_q
    )
    middle = floats + jnp.dot(attended, weight_o, preferred_element_type=jnp.float32)
    inverse2 = inverse_norm(middle)
    unit2 = middle * inverse2
    normed2 = (unit2 * gain2.astype(jnp.float32)).astype(jnp.bfloat16)
    gate_proj = jnp.dot(normed2, weight_gate, preferred_element_type=jnp.float32)
    up_proj = jnp.dot(normed2, weight_up, preferred_element_type=jnp.float32)
    hidden = (jax.nn.silu(gate_proj) * up_proj).astype(jnp.bfloat16)
    result = (middle + jnp.dot(hidden, weight_down, preferred_element_type=jnp.float32)).astype(
        jnp.bfloat16
    )
    saved = (
        positions,
        inverse1,
        unit1,
        normed1,
        queries,
        keys,
        values,
        query_index,
        query_seg,
        outputs,
        log_sums,
        attended,
        inverse2,
        unit2,
        normed2,
        gate_proj,
        up_proj,
        hidden,
    )
    return (result, saved)


def backward_batch(cotan, seq_seg, saved, attn_weights, ffn_weights):
    (
        positions,
        inverse1,
        unit1,
        normed1,
        queries,
        keys,
        values,
        query_index,
        query_seg,
        outputs,
        log_sums,
        attended,
        inverse2,
        unit2,
        normed2,
        gate_proj,
        up_proj,
        hidden,
    ) = saved
    gain1, weight_q, weight_k, weight_v, weight_o = attn_weights
    gain2, weight_gate, weight_up, weight_down = ffn_weights
    tok_rows = cotan.shape[0]
    part_count = lax.axis_size("ulysses")
    head_count = weight_q.shape[1] // HD
    kv_count = weight_k.shape[1] // HD
    group_q = weight_q.shape[1] // part_count
    group_kv = weight_k.shape[1] // part_count
    grad_hidden = jnp.einsum("td,fd->tf", cotan, weight_down, preferred_element_type=jnp.float32)
    gate_sigmoid = jax.nn.sigmoid(gate_proj)
    grad_gate = (
        grad_hidden * up_proj * gate_sigmoid * (1.0 + gate_proj * (1.0 - gate_sigmoid))
    ).astype(jnp.bfloat16)
    grad_up = (grad_hidden * gate_proj * gate_sigmoid).astype(jnp.bfloat16)
    grad_normed2 = jnp.einsum(
        "tf,df->td", grad_gate, weight_gate, preferred_element_type=jnp.float32
    ) + jnp.einsum("tf,df->td", grad_up, weight_up, preferred_element_type=jnp.float32)
    grad_middle = cotan.astype(jnp.float32) + norm_back(
        grad_normed2, gain2.astype(jnp.float32), unit2, inverse2
    )
    grad_attn = grad_middle.astype(jnp.bfloat16)
    grad_attended = jnp.einsum(
        "td,qd->tq", grad_attn, weight_o, preferred_element_type=jnp.float32
    ).astype(jnp.bfloat16)
    grad_sent = lax.all_to_all(
        grad_attended.reshape(tok_rows, part_count, group_q),
        "ulysses",
        split_axis=1,
        concat_axis=0,
        tiled=True,
    )
    grad_out = grad_sent.reshape(queries.shape)
    grad_queries, key_terms = attend_backward(
        queries, keys, values, seq_seg, query_index, query_seg, grad_out, outputs, log_sums
    )
    key_sums = lax.psum_scatter(
        key_terms.astype(jnp.bfloat16), "blk", scatter_dimension=1, tiled=True
    ).astype(jnp.float32)
    back_pack = jnp.concatenate(
        [grad_queries.transpose(0, 3, 1, 2, 4).reshape(part_count, tok_rows, group_q), key_sums],
        axis=2,
    )[:, :, None, :]
    returned = (
        lax.all_to_all(
            back_pack.astype(jnp.bfloat16), "ulysses", split_axis=0, concat_axis=2, tiled=True
        )
        .astype(back_pack.dtype)
        .reshape(tok_rows, part_count, group_q + 2 * group_kv)
    )
    grad_query = (
        rotate(returned[:, :, :group_q].reshape(tok_rows, head_count, HD), positions, -1.0)
        .reshape(tok_rows, head_count * HD)
        .astype(jnp.bfloat16)
    )
    grad_key = (
        rotate(
            returned[:, :, group_q : group_q + group_kv].reshape(tok_rows, kv_count, HD),
            positions,
            -1.0,
        )
        .reshape(tok_rows, kv_count * HD)
        .astype(jnp.bfloat16)
    )
    grad_value = (
        returned[:, :, group_q + group_kv :].reshape(tok_rows, kv_count * HD).astype(jnp.bfloat16)
    )
    grad_normed1 = (
        jnp.einsum("tq,dq->td", grad_query, weight_q, preferred_element_type=jnp.float32)
        + jnp.einsum("tk,dk->td", grad_key, weight_k, preferred_element_type=jnp.float32)
        + jnp.einsum("tk,dk->td", grad_value, weight_v, preferred_element_type=jnp.float32)
    )
    grad_input = grad_middle + norm_back(grad_normed1, gain1.astype(jnp.float32), unit1, inverse1)
    pieces = (
        normed1,
        jnp.concatenate([grad_query, grad_key, grad_value], axis=1),
        attended,
        grad_attn,
        unit1,
        grad_normed1,
        normed2,
        jnp.concatenate([grad_gate, grad_up], axis=1),
        unit2,
        grad_normed2,
        hidden,
        cotan,
    )
    return (grad_input, pieces)


def gain_column(unit_rows, grad_normed, row_count):
    column = jnp.sum(unit_rows * grad_normed, axis=0)
    return jnp.concatenate(
        [column[:, None], jnp.zeros((row_count, gain_block - 1), jnp.float32)], axis=1
    )


def scatter_grads(pieces, width_q, width_kv, hidden_width):
    (
        normed1,
        grad_qkv,
        attended,
        grad_attn,
        unit1,
        grad_normed1,
        normed2,
        grad_gu,
        unit2,
        grad_normed2,
        hidden,
        cotan,
    ) = pieces
    model_width = normed1.shape[1]
    outer_count = lax.axis_size("dp") * lax.axis_size("ulysses")
    projections = jnp.einsum("tc,tk->ck", normed1, grad_qkv, preferred_element_type=jnp.float32)
    output_rows = jnp.einsum("tc,td->cd", attended, grad_attn, preferred_element_type=jnp.float32)
    feed_rows = jnp.einsum("tc,tk->ck", normed2, grad_gu, preferred_element_type=jnp.float32)
    row_part = lax.psum_scatter(
        jnp.concatenate(
            [
                projections,
                output_rows,
                gain_column(
                    unit1,
                    grad_normed1,
                    lax.axis_size(("dp", "ulysses")) * (model_width // outer_count),
                ),
                feed_rows,
                gain_column(
                    unit2,
                    grad_normed2,
                    lax.axis_size(("dp", "ulysses")) * (model_width // outer_count),
                ),
            ],
            axis=1,
        ).astype(jnp.bfloat16),
        ("dp", "ulysses"),
        scatter_dimension=0,
        tiled=True,
    ).astype(jnp.float32)
    down_part = lax.psum_scatter(
        jnp.einsum("tf,td->fd", hidden, cotan, preferred_element_type=jnp.float32).astype(
            jnp.bfloat16
        ),
        ("dp", "ulysses"),
        scatter_dimension=0,
        tiled=True,
    )
    start_o = width_q + 2 * width_kv
    start_gain1 = start_o + model_width
    start_ffn = start_gain1 + gain_block
    start_gain2 = start_ffn + 2 * hidden_width
    part_q = row_part[:, :width_q]
    part_k = row_part[:, width_q : width_q + width_kv]
    part_v = row_part[:, width_q + width_kv : start_o]
    part_o = row_part[:, start_o:start_gain1]
    part_gain1 = row_part[:, start_gain1]
    part_gate = row_part[:, start_ffn : start_ffn + hidden_width]
    part_up = row_part[:, start_ffn + hidden_width : start_gain2]
    part_gain2 = row_part[:, start_gain2]
    return (
        lax.psum_scatter(
            part_gain1.astype(jnp.bfloat16), "blk", scatter_dimension=0, tiled=True
        ).astype(jnp.float32),
        lax.psum_scatter(
            part_q.astype(jnp.bfloat16), "blk", scatter_dimension=1, tiled=True
        ).astype(jnp.float32),
        lax.psum_scatter(
            part_k.astype(jnp.bfloat16), "blk", scatter_dimension=1, tiled=True
        ).astype(jnp.float32),
        lax.psum_scatter(
            part_v.astype(jnp.bfloat16), "blk", scatter_dimension=1, tiled=True
        ).astype(jnp.float32),
        lax.psum_scatter(
            part_o.astype(jnp.bfloat16), "blk", scatter_dimension=1, tiled=True
        ).astype(jnp.float32),
        lax.psum_scatter(
            part_gain2.astype(jnp.bfloat16), "blk", scatter_dimension=0, tiled=True
        ).astype(jnp.float32),
        lax.psum_scatter(
            part_gate.astype(jnp.bfloat16), "blk", scatter_dimension=1, tiled=True
        ).astype(jnp.float32),
        lax.psum_scatter(
            part_up.astype(jnp.bfloat16), "blk", scatter_dimension=1, tiled=True
        ).astype(jnp.float32),
        lax.psum_scatter(down_part, "blk", scatter_dimension=1, tiled=True).astype(jnp.float32),
    )


def shards(tokens, segments, norm1, wq, wk, wv, wo, norm2, w_gate, w_up, w_down, cotangent):
    batch_count = tokens.shape[0]
    seq_seg = lax.all_gather(segments, ("ulysses", "blk"), axis=1, tiled=True)
    shared = gather_layer(norm1, wq, wk, wv, wo, norm2, w_gate, w_up, w_down)
    weight_sets = [shared for batch_index in range(batch_count)]
    results = []
    grad_inputs = []
    piece_lists = []
    for batch_index in range(batch_count):
        layer = weight_sets[batch_index]
        attn_weights = layer[:5]
        ffn_weights = layer[5:]
        result, saved = forward_batch(
            tokens[batch_index],
            segments[batch_index],
            seq_seg[batch_index],
            attn_weights,
            ffn_weights,
        )
        grad_input, pieces = backward_batch(
            cotangent[batch_index], seq_seg[batch_index], saved, attn_weights, ffn_weights
        )
        results.append(result)
        grad_inputs.append(grad_input)
        piece_lists.append(pieces)
    merged = tuple(
        (
            jnp.concatenate([pieces[slot_index] for pieces in piece_lists], axis=0)
            for slot_index in range(len(piece_lists[0]))
        )
    )
    full_layer = weight_sets[0]
    width_q = full_layer[1].shape[1]
    width_kv = full_layer[2].shape[1]
    hidden_width = full_layer[6].shape[1]
    grad_norm1, grad_wq, grad_wk, grad_wv, grad_wo, grad_norm2, grad_gate, grad_up, grad_down = (
        scatter_grads(merged, width_q, width_kv, hidden_width)
    )
    return (
        jnp.stack(results),
        jnp.stack(grad_inputs),
        grad_norm1,
        grad_wq,
        grad_wk,
        grad_wv,
        grad_wo,
        grad_norm2,
        grad_gate,
        grad_up,
        grad_down,
    )


def solution(mesh):
    in_specs = (
        P(None, ("dp", "ulysses", "blk"), None),
        P(None, ("dp", "ulysses", "blk")),
        P(("dp", "ulysses", "blk")),
        P(("dp", "ulysses"), "blk"),
        P(("dp", "ulysses"), "blk"),
        P(("dp", "ulysses"), "blk"),
        P(("dp", "ulysses"), "blk"),
        P(("dp", "ulysses", "blk")),
        P(("dp", "ulysses"), "blk"),
        P(("dp", "ulysses"), "blk"),
        P(("dp", "ulysses"), "blk"),
        P(None, ("dp", "ulysses", "blk"), None),
    )
    out_specs = (
        P(None, ("dp", "ulysses", "blk"), None),
        P(None, ("dp", "ulysses", "blk"), None),
        P(("dp", "ulysses", "blk")),
        P(("dp", "ulysses"), "blk"),
        P(("dp", "ulysses"), "blk"),
        P(("dp", "ulysses"), "blk"),
        P(("dp", "ulysses"), "blk"),
        P(("dp", "ulysses", "blk")),
        P(("dp", "ulysses"), "blk"),
        P(("dp", "ulysses"), "blk"),
        P(("dp", "ulysses"), "blk"),
    )
    return jax.shard_map(shards, mesh=mesh, in_specs=in_specs, out_specs=out_specs, check_vma=False)
```

profile of v0, /device:TPU:0, one launch (start us, length us, event | category | flops | bytes accessed | tf_op | source)
XLA Modules:
  0.0 3472.4 jit_solution(9635795092710680851)
XLA Ops:
  10.6 21.1 all_gather.68
  32.8 21.2 all_gather.70
  60.9 39.1 %all-gather.22.cloned.1.call-done = bf16[320,2560]{1,0:T(8,128)(2,1)} async-done(((bf16[320,640]{1,0:T(8,128)(2,1)}), bf16[320,2560]{1,0:T(8,128)(2,1)}) %all-gather.22.cloned.1.call-update) | async-done | bytes 1638416 | tf_op jit(solution)/shard_map/all_gather | solution.py:47
  100.1 87.9 %all-gather.26.cloned.1.call-done = bf16[320,7168]{1,0:T(8,128)(2,1)} async-done(((bf16[320,1792]{1,0:T(8,128)(2,1)}), bf16[320,7168]{1,0:T(8,128)(2,1)}) %all-gather.26.cloned.1.call-update) | async-done | bytes 4587536 | tf_op jit(solution)/shard_map/all_gather | solution.py:49
  188.1 87.0 %all-gather.30.cloned.1.call-done = bf16[320,7168]{1,0:T(8,128)(2,1)} async-done(((bf16[320,1792]{1,0:T(8,128)(2,1)}), bf16[320,7168]{1,0:T(8,128)(2,1)}) %all-gather.30.cloned.1.call-update) | async-done | bytes 4587536 | tf_op jit(solution)/shard_map/all_gather | solution.py:50
  275.2 87.0 %all-gather.34.cloned.1.call-done = bf16[896,2560]{1,0:T(8,128)(2,1)} async-done(((bf16[896,640]{1,0:T(8,128)(2,1)}), bf16[896,2560]{1,0:T(8,128)(2,1)}) %all-gather.34.cloned.1.call-update) | async-done | bytes 4587536 | tf_op jit(solution)/shard_map/all_gather | solution.py:51
  362.2 18.0 all-gather
  392.1 24.2 all-reduce.7
  441.5 65.7 %all-gather.16.cloned.1.call-done = bf16[2560,2560]{1,0:T(8,128)(2,1)} async-done(((bf16[320,2560]{1,0:T(8,128)(2,1)}), bf16[2560,2560]{1,0:T(8,128)(2,1)}) %all-gather.16.cloned.1.call-update) | async-done | bytes 13107216 | tf_op jit(solution)/shard_map/all_gather | solution.py:55
  507.2 18.1 copy.199
  574.8 17.9 all_gather.83
  680.1 95.4 %all-gather.28.cloned.1.call-done = bf16[2560,7168]{1,0:T(8,128)(2,1)} async-done(((bf16[320,7168]{1,0:T(8,128)(2,1)}), bf16[2560,7168]{1,0:T(8,128)(2,1)}) %all-gather.28.cloned.1.call-update) | async-done | bytes 36700176 | tf_op jit(solution)/shard_map/all_gather | solution.py:60
  775.5 18.9 fusion.243
  794.4 158.1 %all-gather.32.cloned.1.call-done = bf16[2560,7168]{1,0:T(8,128)(2,1)} async-done(((bf16[320,7168]{1,0:T(8,128)(2,1)}), bf16[2560,7168]{1,0:T(8,128)(2,1)}) %all-gather.32.cloned.1.call-update) | async-done | bytes 36700176 | tf_op jit(solution)/shard_map/all_gather | solution.py:61
  952.5 18.7 fusion.244
  1003.6 125.8 %all-gather.36.cloned.1.call-done = bf16[7168,2560]{1,0:T(8,128)(2,1)} async-done(((bf16[896,2560]{1,0:T(8,128)(2,1)}), bf16[7168,2560]{1,0:T(8,128)(2,1)}) %all-gather.36.cloned.1.call-update) | async-done | bytes 36700176 | tf_op jit(solution)/shard_map/all_gather | solution.py:62
  1129.4 20.8 multiply_convert_fusion
  1150.2 20.6 multiply_convert_fusion.2
  1170.8 29.2 convolution_convert_fusion
  1200.0 17.1 fusion.247
  1217.2 17.6 fusion.245
  1234.8 16.8 convolution_add_fusion.10
  1251.6 17.5 multiply_reduce_fusion.5
  1300.3 17.6 copy.251
  1380.1 17.3 reduce-scatter.21.cloned.1.call-done
  1457.7 198.8 %concatenate.156 = bf16[2560,20992]{1,0:T(8,128)(2,1)} concatenate(bf16[2560,3840]{1,0:T(8,128)(2,1)} %convolution_convert_fusion.2, bf16[2560,2560]{1,0:T(8,128)(2,1)} %copy.251, bf16[2560,1]{1,0:T(8,128)(2,1)S(1)} %broadcast_in_dim.203, bf16[2560,127]{1,0:T(8,128)(2,1)S(1)} %broadcast.398, bf16[2560,14336]{1,0:T(8,128)(2,1)} %convolution_convert_fusion, ...), dimensions={1} | concatenate | bytes 214958080 | tf_op jit(solution)/shard_map/concatenate | solution.py:463
  1673.8 1175.3 %all-reduce.12.cloned.1.call-done = bf16[2560,20992]{1,0:T(8,128)(2,1)} async-done(((bf16[2560,20992]{1,0:T(8,128)(2,1)}), bf16[2560,20992]{1,0:T(8,128)(2,1)}) %all-reduce.12.cloned.1.call-update) | async-done | bytes 107479056
  2865.6 208.1 %reduce-scatter.29.cloned.1.call-done = bf16[896,2560]{1,0:T(8,128)(2,1)} async-done(((bf16[7168,2560]{1,0:T(8,128)(2,1)}), bf16[896,2560]{1,0:T(8,128)(2,1)}) %reduce-scatter.29.cloned.1.call-update) | async-done | bytes 4587536 | tf_op jit(solution)/shard_map/reduce_scatter | solution.py:485
  3164.8 41.3 %reduce-scatter.37.cloned.1.call-done = bf16[640,320]{1,0:T(8,128)(2,1)} async-done(((bf16[2560,320]{1,0:T(8,128)(2,1)}), bf16[640,320]{1,0:T(8,128)(2,1)}) %reduce-scatter.37.cloned.1.call-update) | async-done | bytes 409616
  3208.2 82.4 %reduce-scatter.39.cloned.1.call-done = bf16[640,896]{1,0:T(8,128)(2,1)} async-done(((bf16[2560,896]{1,0:T(8,128)(2,1)}), bf16[640,896]{1,0:T(8,128)(2,1)}) %reduce-scatter.39.cloned.1.call-update) | async-done | bytes 1146896
  3294.2 82.4 %reduce-scatter.25.cloned.1.call-done = bf16[320,1792]{1,0:T(8,128)(2,1)} async-done(((bf16[320,7168]{1,0:T(8,128)(2,1)}), bf16[320,1792]{1,0:T(8,128)(2,1)}) %reduce-scatter.25.cloned.1.call-update) | async-done | bytes 1146896 | tf_op jit(solution)/shard_map/reduce_scatter | solution.py:524
  3379.4 83.2 %reduce-scatter.27.cloned.1.call-done = bf16[320,1792]{1,0:T(8,128)(2,1)} async-done(((bf16[320,7168]{1,0:T(8,128)(2,1)}), bf16[320,1792]{1,0:T(8,128)(2,1)}) %reduce-scatter.27.cloned.1.call-update) | async-done | bytes 1146896 | tf_op jit(solution)/shard_map/reduce_scatter | solution.py:527
  (700 shorter events, 564.2 us)
Async XLA Ops:
  7.2 53.6 %all-gather.14.cloned.1.call-start = ((), (), s32[]{:S(2)}) async-start(), calls=%async_computation.18 | async-start | bytes 2048000 | tf_op jit(solution)/shard_map/all_gather | solution.py:44
  7.9 92.1 %all-gather.22.cloned.1.call-start = ((), (), s32[]{:S(2)}) async-start(), calls=%async_computation.22 | async-start | bytes 2048000 | tf_op jit(solution)/shard_map/all_gather | solution.py:47
  8.7 179.3 %all-gather.26.cloned.1.call-start = ((), (), s32[]{:S(2)}) async-start(), calls=%async_computation.24 | async-start | bytes 5734400 | tf_op jit(solution)/shard_map/all_gather | solution.py:49
  9.4 265.7 %all-gather.30.cloned.1.call-start = ((), (), s32[]{:S(2)}) async-start(), calls=%async_computation.26 | async-start | bytes 5734400 | tf_op jit(solution)/shard_map/all_gather | solution.py:50
  10.0 352.2 %all-gather.34.cloned.1.call-start = ((), (), s32[]{:S(2)}) async-start(), calls=%async_computation.28 | async-start | bytes 5734400 | tf_op jit(solution)/shard_map/all_gather | solution.py:51
  10.6 409.1 %all-gather.18.cloned.1.call-start = ((), (), s32[]{:S(2)}) async-start(), calls=%async_computation.20 | async-start | bytes 3686400 | tf_op jit(solution)/shard_map/all_gather | solution.py:56
  32.7 398.4 %all-gather.20.cloned.1.call-start = ((), (), s32[]{:S(2)}) async-start(), calls=%async_computation.21 | async-start | bytes 3686400 | tf_op jit(solution)/shard_map/all_gather | solution.py:57
  54.9 452.2 %all-gather.16.cloned.1.call-start = ((), (), s32[]{:S(2)}) async-start(), calls=%async_computation.19 | async-start | bytes 14745600 | tf_op jit(solution)/shard_map/all_gather | solution.py:55
  60.8 604.5 %all-gather.24.cloned.1.call-start = ((), (), s32[]{:S(2)}) async-start(), calls=%async_computation.23 | async-start | bytes 14745600 | tf_op jit(solution)/shard_map/all_gather | solution.py:58
  100.1 675.5 %all-gather.28.cloned.1.call-start = ((), (), s32[]{:S(2)}) async-start(), calls=%async_computation.25 | async-start | bytes 41287680 | tf_op jit(solution)/shard_map/all_gather | solution.py:60
  188.0 764.5 %all-gather.32.cloned.1.call-start = ((), (), s32[]{:S(2)}) async-start(), calls=%async_computation.27 | async-start | bytes 41287680 | tf_op jit(solution)/shard_map/all_gather | solution.py:61
  275.2 854.2 %all-gather.36.cloned.1.call-start = ((), (), s32[]{:S(2)}) async-start(), calls=%async_computation.29 | async-start | bytes 41287680 | tf_op jit(solution)/shard_map/all_gather | solution.py:62
  537.9 17.9 all-to-all-start.2
  555.8 17.6 all-to-all-start
  559.3 896.4 %copy-start.67 = (f32[2560]{0:T(1024)}, f32[2560]{0:T(1024)S(1)}, u32[]{:S(2)}) copy-start(f32[2560]{0:T(1024)S(1)} %convert_element_type.387) | copy-start | bytes 30724
  611.3 41.0 %all-to-all-start.3 = ((bf16[2,64,1,1280]{3,1,2,0:T(8,128)(2,1)}), bf16[2,64,1,1280]{3,1,2,0:T(8,128)(2,1)}, u32[]{:S(2)}, u32[]{:S(2)}) async-start(bf16[2,64,1,1280]{3,1,2,0:T(8,128)(2,1)} %bitcast.163), calls=%async_computation.3 | async-start | bytes 655360 | tf_op jit(solution)/shard_map/all_to_all | solution.py:289
  652.3 12.6 all-to-all-start.1
  1279.8 39.5 %all-to-all-start.6 = ((bf16[64,2,1280]{2,0,1:T(8,128)(2,1)}), bf16[64,2,1280]{2,0,1:T(8,128)(2,1)}, u32[]{:S(2)}, u32[]{:S(2)}) async-start(bf16[64,2,1280]{2,0,1:T(8,128)(2,1)} %bitcast.624), calls=%async_computation.7 | async-start | bytes 655360 | tf_op jit(solution)/shard_map/all_to_all | solution.py:370
  1319.3 10.0 all-to-all-start.4
  1322.8 51.0 %reduce-scatter.23.cloned.1.call-start = ((), (), s32[]{:S(2)}) async-start(), calls=%async_computation.31 | async-start | bytes 819200 | tf_op jit(solution)/shard_map/reduce_scatter | solution.py:381
  1351.6 45.8 %reduce-scatter.21.cloned.1.call-start = ((), (), s32[]{:S(2)}) async-start(), calls=%async_computation.30 | async-start | bytes 819200 | tf_op jit(solution)/shard_map/reduce_scatter | solution.py:381
  1375.5 23.6 all-to-all-start.7
  1399.2 10.3 all-to-all-start.5
  1403.1 1446.0 %all-reduce.12.cloned.1.call-start = ((), (), s32[]{:S(2)}) async-start(), calls=%async_computation.40 | async-start | bytes 214958080
  1656.5 1417.2 %reduce-scatter.29.cloned.1.call-start = ((), (), s32[]{:S(2)}) async-start(), calls=%async_computation.34 | async-start | bytes 41287680 | tf_op jit(solution)/shard_map/reduce_scatter | solution.py:485
  1673.1 1469.0 %reduce-scatter.33.cloned.1.call-start = ((), (), s32[]{:S(2)}) async-start(), calls=%async_computation.36 | async-start | bytes 614400
  2851.7 292.2 %reduce-scatter.35.cloned.1.call-start = ((), (), s32[]{:S(2)}) async-start(), calls=%async_computation.37 | async-start | bytes 614400
  2852.8 309.7 %reduce-scatter.31.cloned.1.call-start = ((), (), s32[]{:S(2)}) async-start(), calls=%async_computation.35 | async-start | bytes 2457600
  2861.3 344.7 %reduce-scatter.37.cloned.1.call-start = ((), (), s32[]{:S(2)}) async-start(), calls=%async_computation.38 | async-start | bytes 2457600
  2865.5 425.1 %reduce-scatter.39.cloned.1.call-start = ((), (), s32[]{:S(2)}) async-start(), calls=%async_computation.39 | async-start | bytes 5734400
  3081.0 295.7 %reduce-scatter.25.cloned.1.call-start = ((), (), s32[]{:S(2)}) async-start(), calls=%async_computation.32 | async-start | bytes 5734400 | tf_op jit(solution)/shard_map/reduce_scatter | solution.py:524
  3093.3 369.4 %reduce-scatter.27.cloned.1.call-start = ((), (), s32[]{:S(2)}) async-start(), calls=%async_computation.33 | async-start | bytes 5734400 | tf_op jit(solution)/shard_map/reduce_scatter | solution.py:527
  (118 other events, 3613.2 us)
Sparse Core Ops, SparseCore 0:
  9.6 51.1 all-gather.13
  62.4 37.6 all-gather.21
  101.6 86.3 all-gather.25
  189.4 85.6 all-gather.29
  276.5 85.6 all-gather.33
  364.5 31.1 all-gather.17
  398.2 32.8 all-gather.19
  433.0 74.1 all-gather.15
  509.1 83.1 all-gather.23
  594.0 181.4 all-gather.27
  777.4 175.0 all-gather.31
  954.3 175.0 all-gather.35
  1351.7 21.6 reduce-scatter.22
  1376.2 21.1 reduce-scatter.20
  1656.6 1192.3 all-reduce.11
  2852.6 221.0 reduce-scatter.28
  3075.8 21.5 reduce-scatter.32
  3099.6 19.7 reduce-scatter.34
  3122.3 40.1 reduce-scatter.30
  3165.3 40.6 reduce-scatter.36
  3208.3 82.2 reduce-scatter.38
  3293.0 83.6 reduce-scatter.24
  3379.0 83.6 reduce-scatter.26
where the time goes:
time: 3490 us; the launch traced here: 3470 us
  waiting for transfers between devices  2500 us (72%)
  matrix products  366 us (10%)
  local copies, waits for them, and re-layouts  354 us (10%)
  blocking collectives  140 us (4%)
  other arithmetic  48.1 us (1%)
    unnamed x29, waiting for transfers between devices  1320 us
    reduce_scatter x1, waiting for transfers between devices, scatter_grads(): lax.psum_scatter(jnp.einsum('tf,td->fd', hidden, cotan, preferred_element...  208 us
    concatenate x1, local copies, waits for them, and re-layouts, scatter_grads(): jnp.concatenate([projections, output_rows, gain_column(unit1, grad_normed...  199 us
    all_gather x1, waiting for transfers between devices, gather_layer(): lax.all_gather(up_w, ('dp', 'ulysses'), axis=0, tiled=True)  158 us
    all_gather x1, waiting for transfers between devices, gather_layer(): lax.all_gather(down_w, ('dp', 'ulysses'), axis=0, tiled=True)  126 us
    all_gather x1, waiting for transfers between devices, gather_layer(): lax.all_gather(gate_w, ('dp', 'ulysses'), axis=0, tiled=True)  95.4 us
    all_gather x1, waiting for transfers between devices, gather_layer(): lax.all_gather(w_gate, 'blk', axis=1, tiled=True)  87.9 us
    all_gather x1, waiting for transfers between devices, gather_layer(): lax.all_gather(w_up, 'blk', axis=1, tiled=True)  87 us
  transfers between devices with their start and end apart: 31, of which 22 were waited for; matrix products, arithmetic and copies ran while one was open for 10% of the time, Pallas kernels for 0%

commit v1 on v0

--- a/solution.py
+++ b/solution.py
@@ -1,8 +1,11 @@
+import functools
 import math
 
 import jax
 import jax.numpy as jnp
 from jax import lax
+from jax.experimental import pallas as pl
+from jax.experimental.pallas import tpu as pltpu
 from jax.sharding import PartitionSpec as P
 
 HD = 80
@@ -584,6 +587,454 @@
     )
 
 
+def swap_pairs(count, bit):
+    return [(index, index ^ bit) for index in range(count)]
+
+
+def cube_gather(block, axes):
+    for name in axes:
+        count = lax.axis_size(name)
+        bit = 1
+        while bit < count:
+            other = lax.ppermute(block, name, swap_pairs(count, bit))
+            high = (lax.axis_index(name) & bit) != 0
+            block = jnp.concatenate(
+                [jnp.where(high, other, block), jnp.where(high, block, other)], axis=0
+            )
+            bit *= 2
+    return block
+
+
+def cube_scatter(values, axes):
+    for name in axes:
+        count = lax.axis_size(name)
+        bit = count // 2
+        while bit:
+            half = values.shape[0] // 2
+            high = (lax.axis_index(name) & bit) != 0
+            low_half, high_half = values[:half], values[half:]
+            sent = jnp.where(high, low_half, high_half)
+            kept = jnp.where(high, high_half, low_half)
+            values = kept + lax.ppermute(sent, name, swap_pairs(count, bit))
+            bit //= 2
+    return values
+
+
+def ring_pairs(count, direction):
+    return [(index, (index + direction) % count) for index in range(count)]
+
+
+def ring_gather(parts):
+    count = lax.axis_size("blk")
+    slots = [[part] for part in parts]
+    for step in range(count - 1):
+        for m in range(len(parts)):
+            slots[m].append(lax.ppermute(slots[m][-1], "blk", ring_pairs(count, direction_of(m))))
+    return [jnp.concatenate(each, axis=0) for each in slots]
+
+
+def ring_scatter(partials, rows):
+    count = lax.axis_size("blk")
+
+    def piece(m, slot):
+        slot = slot % count
+        return partials[m][slot * rows : (slot + 1) * rows]
+
+    sums = [piece(m, 1) for m in range(len(partials))]
+    for step in range(1, count):
+        for m in range(len(partials)):
+            arrived = lax.ppermute(
+                sums[m].astype(jnp.bfloat16), "blk", ring_pairs(count, direction_of(m))
+            )
+            sums[m] = arrived.astype(jnp.float32) + piece(m, step + 1)
+    return sums
+
+
+def direction_of(m):
+    return 1 if m % 2 == 0 else -1
+
+
+def place_of(index, count):
+    bits = count.bit_length() - 1
+    return int(format(index, f"0{bits}b")[::-1], 2) if bits else 0
+
+
+def cross_pairs(count):
+    return [
+        (d * count + z, place_of(z, count) * count + d) for d in range(count) for z in range(count)
+    ]
+
+
+def cross_back_pairs(count):
+    return [(target, source) for source, target in cross_pairs(count)]
+
+
+def turned(x_ref, padded, cosine, sine):
+    width = x_ref.shape[-1]
+    padded_width = padded.shape[-1]
+    padded[:, :width] = x_ref[...].astype(jnp.float32)
+    whole = padded[...]
+    half = HD // 2
+    lane = lax.broadcasted_iota(jnp.int32, whole.shape, 1)
+    first = lax.rem(lane, HD) < half
+    other = jnp.where(
+        first,
+        pltpu.roll(whole, padded_width - half, 1),
+        pltpu.roll(whole, half, 1),
+    )
+    return padded[:, :width] * cosine + other[:, :width] * sine
+
+
+def turn_kernel(direction, x_ref, cos_ref, sin_ref, out_ref, padded):
+    out_ref[...] = turned(x_ref, padded, cos_ref[...], direction * sin_ref[...]).astype(
+        out_ref.dtype
+    )
+
+
+def turn(values, cosine, sine, direction):
+    rows, width = values.shape
+    block = math.gcd(rows, 256)
+    spec = pl.BlockSpec((block, width), lambda i: (i, 0))
+    return pl.pallas_call(
+        functools.partial(turn_kernel, direction),
+        grid=(rows // block,),
+        in_specs=[spec, spec, spec],
+        out_specs=spec,
+        out_shape=jax.ShapeDtypeStruct((rows, width), jnp.bfloat16),
+        scratch_shapes=[pltpu.VMEM((block, pl.cdiv(width, 128) * 128), jnp.float32)],
+        cost_estimate=pl.CostEstimate(
+            flops=6 * rows * width, bytes_accessed=14 * rows * width, transcendentals=0
+        ),
+    )(values, cosine, sine)
+
+
+def heads_of(ref, first, count):
+    return jnp.concatenate(
+        [ref[0, :, (first + h) * HD : (first + h + 1) * HD] for h in range(count)], axis=0
+    )
+
+
+def mask_of(start_ref, index_ref, key_ref):
+    keys = key_ref[0]
+    seen = (keys >= start_ref[0]) & (keys <= index_ref[0])
+    return jnp.where(seen, 0.0, masked_score)
+
+
+def dot_nt(left, right):
+    return lax.dot_general(left, right, (((1,), (1,)), ((), ())), preferred_element_type=jnp.float32)
+
+
+def dot_tn(left, right):
+    return lax.dot_general(left, right, (((0,), (0,)), ((), ())), preferred_element_type=jnp.float32)
+
+
+def attend_kernel(group, q_ref, k_ref, v_ref, start_ref, index_ref, key_ref, out_ref, log_ref):
+    rows = q_ref.shape[1]
+    kv_count = k_ref.shape[2] // HD
+    mask = mask_of(start_ref, index_ref, key_ref)
+    for kv in range(kv_count):
+        key = k_ref[0, :, kv * HD : (kv + 1) * HD]
+        value = v_ref[0, :, kv * HD : (kv + 1) * HD]
+        for g in range(group):
+            h = kv * group + g
+            query = q_ref[0, :, h * HD : (h + 1) * HD]
+            scores = dot_nt(query, key) * (HD**-0.5) + mask
+            top = jnp.max(scores, axis=1, keepdims=True)
+            weights = jnp.exp(scores - top)
+            total = jnp.sum(weights, axis=1, keepdims=True)
+            mixed = jnp.dot(
+                weights.astype(jnp.bfloat16), value, preferred_element_type=jnp.float32
+            )
+            out_ref[0, :, h * HD : (h + 1) * HD] = (mixed / total).astype(out_ref.dtype)
+            log_ref[0, :, h : h + 1] = top + jnp.log(total)
+
+
+def attend_back_kernel(
+    group,
+    q_ref,
+    k_ref,
+    v_ref,
+    start_ref,
+    index_ref,
+    key_ref,
+    log_ref,
+    grad_ref,
+    gq_ref,
+    gk_ref,
+    gv_ref,
+):
+    kv_count = k_ref.shape[2] // HD
+    scale = HD**-0.5
+    mask = mask_of(start_ref, index_ref, key_ref)
+    for kv in range(kv_count):
+        key = k_ref[0, :, kv * HD : (kv + 1) * HD]
+        value = v_ref[0, :, kv * HD : (kv + 1) * HD]
+        grad_key = None
+        grad_value = None
+        for g in range(group):
+            h = kv * group + g
+            query = q_ref[0, :, h * HD : (h + 1) * HD]
+            grad = grad_ref[0, :, h * HD : (h + 1) * HD]
+            scores = dot_nt(query, key) * scale + mask
+            probs = jnp.exp(scores - log_ref[0, :, h : h + 1])
+            grad_probs = dot_nt(grad, value)
+            delta = jnp.sum(probs * grad_probs, axis=1, keepdims=True)
+            grad_scores = (probs * (grad_probs - delta)).astype(jnp.bfloat16)
+            gq_ref[0, :, h * HD : (h + 1) * HD] = (
+                jnp.dot(grad_scores, key, preferred_element_type=jnp.float32) * scale
+            )
+            key_term = dot_tn(grad_scores, query)
+            value_term = dot_tn(probs.astype(jnp.bfloat16), grad)
+            grad_key = key_term if grad_key is None else grad_key + key_term
+            grad_value = value_term if grad_value is None else grad_value + value_term
+        gk_ref[0, :, kv * HD : (kv + 1) * HD] = grad_key * scale
+        gv_ref[0, :, kv * HD : (kv + 1) * HD] = grad_value
+
+
+def whole_block(shape):
+    return pl.BlockSpec((1,) + shape[1:], lambda m: (m,) + (0,) * (len(shape) - 1))
+
+
+def attend_call(kernel, operands, outs, flops, exps):
+    return pl.pallas_call(
+        kernel,
+        grid=(operands[0].shape[0],),
+        in_specs=[whole_block(each.shape) for each in operands],
+        out_specs=[whole_block(each.shape) for each in outs],
+        out_shape=outs,
+        cost_estimate=pl.CostEstimate(
+            flops=flops,
+            bytes_accessed=sum(each.size * each.dtype.itemsize for each in (*operands, *outs)),
+            transcendentals=exps,
+        ),
+    )(*operands)
+
+
+def matmul(left, right):
+    return jnp.dot(left, right, preferred_element_type=jnp.float32)
+
+
+def matmul_nt(left, right):
+    return jnp.einsum("tc,dc->td", left, right, preferred_element_type=jnp.float32)
+
+
+def grad_of(left, right):
+    return jnp.einsum("tc,td->cd", left, right, preferred_element_type=jnp.float32).astype(
+        jnp.bfloat16
+    )
+
+
+def split_shards(
+    tokens, segments, norm1, wq, wk, wv, wo, norm2, w_gate, w_up, w_down, cotangent
+):
+    batch_count, tok_rows, width = tokens.shape
+    n_dp, n_u, n_z = (lax.axis_size(name) for name in ("dp", "ulysses", "blk"))
+    u_id, z_id = lax.axis_index("ulysses"), lax.axis_index("blk")
+    bf16, f32 = jnp.bfloat16, jnp.float32
+    outer = ("dp", "ulysses")
+    part_len = n_z * tok_rows
+    seq_len = n_u * part_len
+    group_rows = batch_count * part_len
+    q_width, kv_width = wq.shape[1], wk.shape[1]
+    group = q_width // kv_width
+    gain_rows = norm1.shape[0]
+    block_of = [place_of(z, n_z) for z in range(n_z)]
+
+    own_wo, own_down = (lax.ppermute(w, ("dp", "blk"), cross_pairs(n_z)) for w in (wo, w_down))
+    qkv_w = lax.all_gather(jnp.concatenate([wq, wk, wv], axis=1), outer, axis=0, tiled=True)
+    wo_all = lax.all_gather(own_wo, outer, axis=0, tiled=True)
+    gate_w = lax.all_gather(w_gate, outer, axis=0, tiled=True)
+    up_w = lax.all_gather(w_up, outer, axis=0, tiled=True)
+    down_all = lax.all_gather(own_down, outer, axis=0, tiled=True)
+    wo_rows, down_rows = n_u * wo.shape[0], n_u * w_down.shape[0]
+    wo_blocks = [wo_all[block_of[z] * wo_rows :][:wo_rows] for z in range(n_z)]
+    down_blocks = [down_all[block_of[z] * down_rows :][:down_rows] for z in range(n_z)]
+
+    small = jnp.concatenate([norm1, norm2, segments.reshape(-1).astype(bf16)])[None]
+    small = cube_gather(small, ("blk", "ulysses"))
+    seg_blocks = (
+        small[:, 2 * gain_rows :].astype(jnp.int32).reshape(n_u * n_z, batch_count, tok_rows)
+    )
+    seq_seg = seg_blocks.transpose(1, 0, 2).reshape(batch_count, seq_len)
+    small = cube_gather(small, ("dp",))
+    gain1 = small[:, :gain_rows].reshape(1, width).astype(f32)
+    gain2 = small[:, gain_rows : 2 * gain_rows].reshape(1, width).astype(f32)
+
+    slots = jnp.arange(n_z, dtype=jnp.int32)
+    slot_z = jnp.stack([(z_id - direction_of(m) * slots) % n_z for m in range(batch_count)])
+    in_part = (
+        slot_z[:, :, None] * tok_rows + jnp.arange(tok_rows, dtype=jnp.int32)[None, None, :]
+    ).reshape(batch_count, part_len)
+    index = u_id * part_len + in_part
+    chosen = (
+        (u_id * n_z + slot_z)[:, :, None] == jnp.arange(n_u * n_z, dtype=jnp.int32)[None, None, :]
+    ).astype(jnp.int32)
+    own_seg = jnp.sum(
+        chosen[:, :, :, None] * seq_seg.reshape(batch_count, 1, n_u * n_z, tok_rows), axis=2
+    ).reshape(batch_count, part_len)
+    start = jnp.sum((seq_seg[:, None, :] < own_seg[:, :, None]).astype(jnp.int32), axis=2)
+    position = (index - start).reshape(group_rows)
+    half = HD // 2
+    inverse_freq = rope_base ** (-2.0 * jnp.arange(half, dtype=f32) / HD)
+    angles = position.astype(f32)[:, None] * inverse_freq[None, :]
+    cosine, sine = lax.optimization_barrier((jnp.cos(angles), jnp.sin(angles)))
+    turning = (q_width + kv_width) // HD
+    cos_all = jnp.concatenate(
+        [cosine, cosine] * turning + [jnp.ones((group_rows, kv_width), f32)], axis=1
+    )
+    sin_all = jnp.concatenate(
+        [-sine, sine] * turning + [jnp.zeros((group_rows, kv_width), f32)], axis=1
+    )
+    cos_all, sin_all = lax.optimization_barrier((cos_all, sin_all))
+    key_index = jnp.concatenate(
+        [index] + [((u_id - step) % n_u) * part_len + in_part for step in range(1, n_u)], axis=1
+    )
+    start_col, index_col, key_row = start[:, :, None], index[:, :, None], key_index[:, None, :]
+
+    def batches(array):
+        return [array[m * part_len : (m + 1) * part_len] for m in range(batch_count)]
+
+    def gathered(array):
+        return jnp.concatenate(ring_gather([array[m] for m in range(batch_count)]), axis=0)
+
+    def scattered(partial):
+        return jnp.stack(ring_scatter(batches(partial), tok_rows))
+
+    group_tokens = gathered(tokens)
+    group_floats = group_tokens.astype(f32)
+    unit1_group = group_floats * inverse_norm(group_floats)
+    normed1 = (unit1_group * gain1).astype(bf16)
+    qkv = turn(matmul(normed1, qkv_w), cos_all, sin_all, 1.0)
+    qkv = qkv.reshape(batch_count, part_len, q_width + 2 * kv_width)
+    queries = qkv[:, :, :q_width]
+    own_kv = qkv[:, :, q_width:]
+    kv_parts = [own_kv]
+    for step in range(1, n_u):
+        kv_parts.append(
+            lax.ppermute(own_kv, "ulysses", [(i, i + step) for i in range(n_u - step)])
+        )
+    all_kv = jnp.concatenate(kv_parts, axis=1)
+    keys, values = all_kv[:, :, :kv_width], all_kv[:, :, kv_width:]
+    heads = q_width // HD
+    products = 2 * batch_count * heads * part_len * seq_len * HD
+    exps = batch_count * heads * part_len * seq_len
+    attended, log_sums = attend_call(
+        functools.partial(attend_kernel, group),
+        (queries, keys, values, start_col, index_col, key_row),
+        (
+            jax.ShapeDtypeStruct(queries.shape, bf16),
+            jax.ShapeDtypeStruct((batch_count, part_len, heads), f32),
+        ),
+        2 * products,
+        exps,
+    )
+    attended = attended.reshape(group_rows, q_width)
+    mixed = jnp.concatenate([matmul(attended, block) for block in wo_blocks], axis=1)
+    floats = tokens.astype(f32)
+    middle = floats + scattered(mixed)
+    inverse2 = inverse_norm(middle)
+    unit2 = middle * inverse2
+    normed2 = gathered((unit2 * gain2[None]).astype(bf16))
+    group_cotan = gathered(cotangent)
+    gate_proj = matmul(normed2, gate_w)
+    up_proj = matmul(normed2, up_w)
+    hidden = (jax.nn.silu(gate_proj) * up_proj).astype(bf16)
+    ffn = jnp.concatenate([matmul(hidden, block) for block in down_blocks], axis=1)
+    result = (middle + scattered(ffn)).astype(bf16)
+
+    cotan_cols = [group_cotan[:, z * w_down.shape[1] :][:, : w_down.shape[1]] for z in range(n_z)]
+    grad_hidden = sum(matmul_nt(cotan_cols[z], down_blocks[z]) for z in range(n_z))
+    gate_sigmoid = jax.nn.sigmoid(gate_proj)
+    grad_gate = (
+        grad_hidden * up_proj * gate_sigmoid * (1.0 + gate_proj * (1.0 - gate_sigmoid))
+    ).astype(bf16)
+    grad_up = (grad_hidden * gate_proj * gate_sigmoid).astype(bf16)
+    order = sorted(range(n_z), key=lambda z: block_of[z])
+
+    def reduced(grads):
+        return lax.psum_scatter(grads, outer, scatter_dimension=0, tiled=True)
+
+    def returned(grads):
+        return lax.ppermute(reduced(grads), ("dp", "blk"), cross_back_pairs(n_z))
+
+    down_grad = returned(
+        jnp.concatenate([grad_of(hidden, cotan_cols[z]) for z in order], axis=0)
+    )
+    gate_grad = reduced(grad_of(normed2, grad_gate))
+    up_grad = reduced(grad_of(normed2, grad_up))
+    grad_normed2 = scattered(matmul_nt(grad_gate, gate_w) + matmul_nt(grad_up, up_w))
+    grad_middle = cotangent.astype(f32) + norm_back(grad_normed2, gain2[None], unit2, inverse2)
+    grad_attn = gathered(grad_middle.astype(bf16))
+    attn_cols = [grad_attn[:, z * wo.shape[1] :][:, : wo.shape[1]] for z in range(n_z)]
+    wo_grad = returned(jnp.concatenate([grad_of(attended, attn_cols[z]) for z in order], axis=0))
+    grad_attended = sum(matmul_nt(attn_cols[z], wo_blocks[z]) for z in range(n_z)).astype(bf16)
+    grad_q, grad_k, grad_v = attend_call(
+        functools.partial(attend_back_kernel, group),
+        (
+            queries,
+            keys,
+            values,
+            start_col,
+            index_col,
+            key_row,
+            log_sums,
+            grad_attended.reshape(queries.shape),
+        ),
+        (
+            jax.ShapeDtypeStruct(queries.shape, f32),
+            jax.ShapeDtypeStruct(keys.shape, f32),
+            jax.ShapeDtypeStruct(values.shape, f32),
+        ),
+        5 * products,
+        exps,
+    )
+    grad_kv = jnp.concatenate([grad_k, grad_v], axis=2)
+    own_grad_kv = grad_kv[:, :part_len]
+    for step in range(1, n_u):
+        arrived = lax.ppermute(
+            grad_kv[:, step * part_len : (step + 1) * part_len].astype(bf16),
+            "ulysses",
+            [(i + step, i) for i in range(n_u - step)],
+        )
+        own_grad_kv = own_grad_kv + arrived.astype(f32)
+    grad_qkv = jnp.concatenate([grad_q, own_grad_kv], axis=2).reshape(
+        group_rows, q_width + 2 * kv_width
+    )
+    grad_qkv = turn(grad_qkv, cos_all, sin_all, -1.0)
+    qkv_grad = reduced(grad_of(normed1, grad_qkv))
+    partial1 = matmul_nt(grad_qkv, qkv_w)
+    grad_normed1 = scattered(partial1)
+    inverse1 = inverse_norm(floats)
+    grad_input = grad_middle + norm_back(grad_normed1, gain1[None], floats * inverse1, inverse1)
+    gain_grads = jnp.stack(
+        [
+            jnp.sum(unit1_group * partial1, axis=0),
+            jnp.sum(unit2 * grad_normed2, axis=(0, 1)),
+        ],
+        axis=1,
+    )
+    gain_grads = cube_scatter(gain_grads, ("dp", "ulysses", "blk"))
+    qkv_grad = qkv_grad.astype(f32)
+    return (
+        result,
+        grad_input,
+        gain_grads[:, 0],
+        qkv_grad[:, :q_width],
+        qkv_grad[:, q_width : q_width + kv_width],
+        qkv_grad[:, q_width + kv_width :],
+        wo_grad.astype(f32),
+        gain_grads[:, 1],
+        gate_grad.astype(f32),
+        up_grad.astype(f32),
+        down_grad.astype(f32),
+    )
+
+
+def splits_evenly(mesh):
+    sizes = [mesh.shape[name] for name in ("dp", "ulysses", "blk")]
+    return mesh.shape["dp"] == mesh.shape["blk"] and all(size & (size - 1) == 0 for size in sizes)
+
+
 def solution(mesh):
     in_specs = (
         P(None, ("dp", "ulysses", "blk"), None),
@@ -612,4 +1063,5 @@
         P(("dp", "ulysses"), "blk"),
         P(("dp", "ulysses"), "blk"),
     )
-    return jax.shard_map(shards, mesh=mesh, in_specs=in_specs, out_specs=out_specs, check_vma=False)
+    body = split_shards if splits_evenly(mesh) else shards
+    return jax.shard_map(body, mesh=mesh, in_specs=in_specs, out_specs=out_specs, check_vma=False)

time: 3490 us -> 833 us (0.24)
  waiting for transfers between devices: 2500 us -> 375 us
  local copies, waits for them, and re-layouts: 354 us -> 47 us
  matrix products: 366 us -> 148 us
  blocking collectives: 140 us -> 0 us
  starting transfers between devices: 31.1 us -> 164 us
    unnamed x29 -> x10, waiting for transfers between devices: 1320 us -> 1.33 us
    all_gather x12 -> x5, waiting for transfers between devices: 755 us -> 0.04 us  [the longest x1 0.02 us: split_shards(): wo_all = lax.all_gather(own_wo, outer, axis=0, tiled=True)]
    reduce_scatter x5, waiting for transfers between devices: 391 us -> 74 us  [reduced(): return lax.psum_scatter(grads, outer, scatter_dimension=0, tiled=True)]
    ppermute x0 -> x64, waiting for transfers between devices: none -> 300 us  [the longest x24 130 us: ring_gather(): lax.ppermute(slots[m][-1], 'blk', ring_pairs(count, direction_of(m)))]
    dot_general x74 -> x33, matrix products: 366 us -> 148 us  [the longest x11 58 us: matmul_nt(): jnp.einsum('tc,dc->td', left, right, preferred_element_type=jnp.float32)]
    concatenate x15 -> x6, local copies, waits for them, and re-layouts: 206 us -> 9.53 us  [the longest x4 3.26 us: gathered(): jnp.concatenate(ring_gather([array[m] for m in range(batch_count)]), axis=0)]
    ppermute x0 -> x64, starting transfers between devices: none -> 162 us  [the longest x24 66.2 us: ring_gather(): lax.ppermute(slots[m][-1], 'blk', ring_pairs(count, direction_of(m)))]
    all_gather x5 -> x0, blocking collectives: 94.7 us -> none  [the longest x2 34.4 us: forward_batch(): lax.all_gather(local_kv, 'blk', axis=1, tiled=True)]
  transfers between devices with their start and end apart: 31 -> 74, of which waited for: 22 -> 41; matrix products, arithmetic and copies ran while one was open for 10% -> 24% of each run, Pallas kernels for 0% -> 4%
where the time goes in v1:
time: 833 us; the launch traced here: 825 us
  waiting for transfers between devices  375 us (45%)
  starting transfers between devices  164 us (20%)
  matrix products  148 us (18%)
  local copies, waits for them, and re-layouts  47 us (6%)
  other arithmetic  46.2 us (6%)
  Pallas kernels  29.7 us (4%)
  between operations  15.5 us (2%)
    ppermute x24, waiting for transfers between devices, ring_gather(): lax.ppermute(slots[m][-1], 'blk', ring_pairs(count, direction_of(m)))  130 us
    ppermute x24, waiting for transfers between devices, ring_scatter(): lax.ppermute(sums[m].astype(jnp.bfloat16), 'blk', ring_pairs(count, direc...  122 us
    reduce_scatter x5, waiting for transfers between devices, reduced(): return lax.psum_scatter(grads, outer, scatter_dimension=0, tiled=True)  74 us
    ppermute x24, starting transfers between devices, ring_gather(): lax.ppermute(slots[m][-1], 'blk', ring_pairs(count, direction_of(m)))  66.2 us
    dot_general x11, matrix products, matmul_nt(): jnp.einsum('tc,dc->td', left, right, preferred_element_type=jnp.float32)  58 us
    dot_general x11, matrix products, matmul(): return jnp.dot(left, right, preferred_element_type=jnp.float32)  50.2 us
    ppermute x24, starting transfers between devices, ring_scatter(): lax.ppermute(sums[m].astype(jnp.bfloat16), 'blk', ring_pairs(count, direc...  46.3 us
    dot_general x11, matrix products, grad_of(): jnp.einsum('tc,td->cd', left, right, preferred_element_type=jnp.float32)  39.3 us
  transfers between devices with their start and end apart: 74, of which 41 were waited for; matrix products, arithmetic and copies ran while one was open for 24% of the time, Pallas kernels for 4%

profile of v1, /device:TPU:0, one launch (start us, length us, event | category | flops | bytes accessed | tf_op | source)
XLA Modules:
  0.0 824.9 jit_solution(2374081111451341457)
XLA Ops:
  14.6 15.0 %collective-permute-start.6 = (bf16[1,288]{1,0:T(2,128)(2,1)S(1)}, bf16[1,288]{1,0:T(2,128)(2,1)S(1)}, u32[]{:S(2)}, u32[]{:S(2)}) collective-permute-start(bf16[1,288]{1,0:T(2,128)(2,1)S(1)} %broadcast_in_dim.10), channel_id=1, source_target_pairs={{0,1},{1,0},{2,3},{3,2},{4,5},{5,4},{6,7},{7,6},{8,9},{9,8},{10,11... | collective-permute-start | bytes 1736 | tf_op jit(solution)/shard_map/ppermute | solution.py:599
  30.4 9.7 %collective-permute-start.35 = (bf16[64,2560]{1,0:T(8,128)(2,1)}, bf16[64,2560]{1,0:T(8,128)(2,1)}, u32[]{:S(2)}, u32[]{:S(2)}) collective-permute-start(bf16[64,2560]{1,0:T(8,128)(2,1)} %get-tuple-element.130), channel_id=1, source_target_pairs={{0,3},{1,0},{2,1},{3,2},{4,7},{5,4},{6,5},{7,6},{8,11},{9,8},{10,9... | collective-permute-start | bytes 983048 | tf_op jit(solution)/shard_map/ppermute | solution.py:632
  48.3 19.5 %collective-permute-done.7 = bf16[2,288]{1,0:T(2,128)(2,1)S(1)} collective-permute-done((bf16[2,288]{1,0:T(2,128)(2,1)S(1)}, bf16[2,288]{1,0:T(2,128)(2,1)S(1)}, u32[]{:S(2)}, u32[]{:S(2)}) %collective-permute-start.7) | collective-permute-done | bytes 1184 | tf_op jit(solution)/shard_map/ppermute | solution.py:599
  98.6 51.9 %collective-permute-done.36 = bf16[64,2560]{1,0:T(8,128)(2,1)} collective-permute-done((bf16[64,2560]{1,0:T(8,128)(2,1)}, bf16[64,2560]{1,0:T(8,128)(2,1)}, u32[]{:S(2)}, u32[]{:S(2)}) %collective-permute-start.36) | collective-permute-done | bytes 327712 | tf_op jit(solution)/shard_map/ppermute | solution.py:632
  150.5 11.8 %collective-permute-start.34 = (bf16[64,2560]{1,0:T(8,128)(2,1)S(1)}, bf16[64,2560]{1,0:T(8,128)(2,1)S(1)}, u32[]{:S(2)}, u32[]{:S(2)}) collective-permute-start(bf16[64,2560]{1,0:T(8,128)(2,1)S(1)} %collective-permute-done.33), channel_id=1, source_target_pairs={{0,1},{1,2},{2,3},{3,0},{4,5},{5,6},{6,7},{7,4},{8,9},{9,10},{10,1... | collective-permute-start | bytes 983048 | tf_op jit(solution)/shard_map/ppermute | solution.py:632
  162.8 9.2 %collective-permute-start.2 = (bf16[64,2560]{1,0:T(8,128)(2,1)S(1)}, bf16[64,2560]{1,0:T(8,128)(2,1)S(1)}, u32[]{:S(2)}, u32[]{:S(2)}) collective-permute-start(bf16[64,2560]{1,0:T(8,128)(2,1)S(1)} %collective-permute-done.1), channel_id=1, source_target_pairs={{0,1},{1,2},{2,3},{3,0},{4,5},{5,6},{6,7},{7,4},{8,9},{9,10},{10,1... | collective-permute-start | bytes 983048 | tf_op jit(solution)/shard_map/ppermute | solution.py:632
  173.4 16.4 %collective-permute-done.2 = bf16[64,2560]{1,0:T(8,128)(2,1)S(1)} collective-permute-done((bf16[64,2560]{1,0:T(8,128)(2,1)S(1)}, bf16[64,2560]{1,0:T(8,128)(2,1)S(1)}, u32[]{:S(2)}, u32[]{:S(2)}) %collective-permute-start.2) | collective-permute-done | bytes 327712 | tf_op jit(solution)/shard_map/ppermute | solution.py:632
  218.4 10.2 %collective-permute-done.11 = bf16[2,256,320]{2,1,0:T(8,128)(2,1)S(1)} collective-permute-done((bf16[2,256,320]{2,1,0:T(8,128)(2,1)S(1)}, bf16[2,256,320]{2,1,0:T(8,128)(2,1)S(1)}, u32[]{:S(2)}, u32[]{:S(2)}) %collective-permute-start.11) | collective-permute-done | bytes 327712 | tf_op jit(solution)/shard_map/ppermute | solution.py:914
  229.8 8.0 shard_map.204
  248.5 8.0 collective-permute-done.13
  296.9 9.5 %collective-permute-done.22 = bf16[64,2560]{1,0:T(8,128)(2,1)S(1)} collective-permute-done((bf16[64,2560]{1,0:T(8,128)(2,1)S(1)}, bf16[64,2560]{1,0:T(8,128)(2,1)S(1)}, u32[]{:S(2)}, u32[]{:S(2)}) %collective-permute-start.22) | collective-permute-done | bytes 327712 | tf_op jit(solution)/shard_map/ppermute | solution.py:632
  339.7 11.1 %fusion.115 = f32[512,1792]{1,0:T(8,128)} fusion(bf16[512,2560]{1,0:T(8,128)(2,1)} %constant_dynamic-update-slice_fusion.8, bf16[2560,1792]{1,0:T(8,128)(2,1)} %all-gather.12.cloned.1.call-done), kind=kOutput, calls=%fused_computation.276 | convolution fusion | flops 4697620480 | bytes 15466496 | tf_op jit(solution)/shard_map/dot_general | solution.py:814
  350.8 11.1 %fusion.114 = f32[512,1792]{1,0:T(8,128)} fusion(bf16[512,2560]{1,0:T(8,128)(2,1)} %constant_dynamic-update-slice_fusion.8, bf16[2560,1792]{1,0:T(8,128)(2,1)} %all-gather.10.cloned.1.call-done), kind=kOutput, calls=%fused_computation.275 | convolution fusion | flops 4697620480 | bytes 15466496 | tf_op jit(solution)/shard_map/dot_general | solution.py:814
  374.6 8.5 %multiply_convert_fusion = (bf16[512,1792]{1,0:T(8,128)(2,1)}, bf16[512,1792]{1,0:T(8,128)(2,1)}, bf16[512,1792]{1,0:T(8,128)(2,1)S(1)}) fusion(f32[512,1792]{1,0:T(8,128)} %fusion.114, f32[512,1792]{1,0:T(8,128)} %fusion.115, bf16[7168,640]{1,0:T(8,128)(2,1)S(1)} %bitcast.113, bf16[512,2560]{1,0:T(8,128)(2,1)S(1)} %copy-done.18, ...), kind=kOutput, calls=%fused_computation.14 | convolution fusion | flops 1191837696 | bytes 26804224 | tf_op jit(solution)/shard_map/tc,dc->td/dot_general | solution.py:818
  394.4 11.5 %fusion.116 = f32[512,2560]{1,0:T(8,128)} fusion(bf16[512,1792]{1,0:T(8,128)(2,1)} %get-tuple-element.89, bf16[2560,1792]{1,0:T(8,128)(2,1)} %all-gather.10.cloned.1.call-done), kind=kOutput, calls=%fused_computation.277 | convolution fusion | flops 4697620480 | bytes 16252928 | tf_op jit(solution)/shard_map/tc,dc->td/dot_general | solution.py:818
  405.9 13.3 %fusion.113 = (bf16[512,2560]{1,0:T(8,128)(2,1)S(1)}, f32[512,2560]{1,0:T(8,128)S(1)}) fusion(f32[512,2560]{1,0:T(8,128)} %fusion.116, bf16[512,1792]{1,0:T(8,128)(2,1)} %get-tuple-element.88, bf16[2560,1792]{1,0:T(8,128)(2,1)} %all-gather.12.cloned.1.call-done), kind=kOutput, calls=%fused_computation.274 | convolution fusion | flops 4700241920 | bytes 24117248 | tf_op jit(solution)/shard_map/tc,dc->td/dot_general | solution.py:818
  423.0 8.1 collective-permute-done.38
  437.6 8.6 %collective-permute-done.39 = bf16[64,2560]{1,0:T(8,128)(2,1)S(1)} collective-permute-done((bf16[64,2560]{1,0:T(8,128)(2,1)S(1)}, bf16[64,2560]{1,0:T(8,128)(2,1)S(1)}, u32[]{:S(2)}, u32[]{:S(2)}) %collective-permute-start.39) | collective-permute-done | bytes 327712 | tf_op jit(solution)/shard_map/ppermute | solution.py:646
  454.5 8.6 %collective-permute-done.40 = bf16[64,2560]{1,0:T(8,128)(2,1)S(1)} collective-permute-done((bf16[64,2560]{1,0:T(8,128)(2,1)S(1)}, bf16[64,2560]{1,0:T(8,128)(2,1)S(1)}, u32[]{:S(2)}, u32[]{:S(2)}) %collective-permute-start.40) | collective-permute-done | bytes 327712 | tf_op jit(solution)/shard_map/ppermute | solution.py:646
  470.4 8.1 collective-permute-done.47
  502.3 11.7 %collective-permute-done.46 = bf16[64,2560]{1,0:T(8,128)(2,1)S(1)} collective-permute-done((bf16[64,2560]{1,0:T(8,128)(2,1)S(1)}, bf16[64,2560]{1,0:T(8,128)(2,1)S(1)}, u32[]{:S(2)}, u32[]{:S(2)}) %collective-permute-start.46) | collective-permute-done | bytes 327712 | tf_op jit(solution)/shard_map/ppermute | solution.py:632
  517.1 8.8 %pad_maximum_fusion.3 = bf16[2560,640]{1,0:T(8,128)(2,1)} fusion(bf16[640,640]{1,0:T(8,128)(2,1)S(1)} %convolution_convert_fusion.7, bf16[640,640]{1,0:T(8,128)(2,1)S(1)} %convolution_convert_fusion.8, bf16[640,640]{1,0:T(8,128)(2,1)S(1)} %convolution_convert_fusion.9, bf16[640,640]{1,0:T(8,128)(2,1)S(1)} %convolution_convert_fusion.10), kind=kLoop, calls=%fused_computation.19 | loop fusion | flops 13107200 | bytes 6553600 | tf_op jit(solution)/shard_map/concatenate | solution.py:969
  535.5 12.6 %shard_map.205 = (f32[2,256,640]{2,1,0:T(8,128)}, f32[2,512,160]{2,1,0:T(8,128)}, f32[2,512,160]{2,1,0:T(8,128)}) custom-call(bf16[2,256,640]{2,1,0:T(8,128)(2,1)} %slice.387.q_ref, bf16[2,512,160]{2,1,0:T(8,128)(2,1)} %get-tuple-element.124.k_ref, bf16[2,512,160]{2,1,0:T(8,128)(2,1)} %get-tuple-element.123.v_ref, s32[2,256,1]{2,1,0:T(8,128)} %copy.64.start_ref, ...), custom_call_target="tpu_custom_call" | custom-call | flops 1677721600 | bytes 4612096 | tf_op jit(solution)/shard_map/pallas_call | solution.py:799
  550.9 14.7 %collective-permute-done.50 = bf16[2,256,320]{2,1,0:T(8,128)(2,1)S(1)} collective-permute-done((bf16[2,256,320]{2,1,0:T(8,128)(2,1)S(1)}, bf16[2,256,320]{2,1,0:T(8,128)(2,1)S(1)}, u32[]{:S(2)}, u32[]{:S(2)}) %collective-permute-start.50) | collective-permute-done | bytes 327712 | tf_op jit(solution)/shard_map/ppermute | solution.py:994
  579.7 10.9 %convolution_convert_fusion = bf16[2560,1792]{1,0:T(8,128)(2,1)} fusion(bf16[512,2560]{1,0:T(8,128)(2,1)} %constant_dynamic-update-slice_fusion.8, bf16[512,1792]{1,0:T(8,128)(2,1)} %get-tuple-element.88), kind=kOutput, calls=%fused_computation | convolution fusion | flops 4702208000 | bytes 13631488 | tf_op jit(solution)/shard_map/tc,td->cd/dot_general | solution.py:822
  590.7 11.6 %convolution_convert_fusion.1 = bf16[2560,1792]{1,0:T(8,128)(2,1)} fusion(bf16[512,2560]{1,0:T(8,128)(2,1)} %constant_dynamic-update-slice_fusion.8, bf16[512,1792]{1,0:T(8,128)(2,1)} %get-tuple-element.89), kind=kOutput, calls=%fused_computation.1 | convolution fusion | flops 4702208000 | bytes 13631488 | tf_op jit(solution)/shard_map/tc,td->cd/dot_general | solution.py:822
  632.8 10.5 %collective-permute-done.27 = bf16[64,2560]{1,0:T(8,128)(2,1)S(1)} collective-permute-done((bf16[64,2560]{1,0:T(8,128)(2,1)S(1)}, bf16[64,2560]{1,0:T(8,128)(2,1)S(1)}, u32[]{:S(2)}, u32[]{:S(2)}) %collective-permute-start.27) | collective-permute-done | bytes 327712 | tf_op jit(solution)/shard_map/ppermute | solution.py:646
  651.3 9.0 %collective-permute-start.57 = (f32[1280,2]{0,1:T(2,128)S(1)}, f32[1280,2]{0,1:T(2,128)S(1)}, u32[]{:S(2)}, u32[]{:S(2)}) collective-permute-start(f32[1280,2]{0,1:T(2,128)S(1)} %broadcast_select_fusion.2), channel_id=1, source_target_pairs={{0,16},{8,24},{16,0},{24,8},{1,17},{9,25},{17,1},{25,9},{2,18},{10... | collective-permute-start | bytes 30728 | tf_op jit(solution)/shard_map/ppermute | solution.py:618
  686.5 8.4 %collective-permute-done.52 = bf16[64,2560]{1,0:T(8,128)(2,1)S(1)} collective-permute-done((bf16[64,2560]{1,0:T(8,128)(2,1)S(1)}, bf16[64,2560]{1,0:T(8,128)(2,1)S(1)}, u32[]{:S(2)}, u32[]{:S(2)}) %collective-permute-start.52) | collective-permute-done | bytes 327712 | tf_op jit(solution)/shard_map/ppermute | solution.py:646
  702.3 8.0 collective-permute-done.53
  714.9 10.3 %collective-permute-start.63 = (bf16[896,640]{1,0:T(8,128)(2,1)}, bf16[896,640]{1,0:T(8,128)(2,1)}, u32[]{:S(2)}, u32[]{:S(2)}) collective-permute-start(bf16[896,640]{1,0:T(8,128)(2,1)} %reduce-scatter.14.cloned.1.call-done), channel_id=1, source_target_pairs={{0,0},{16,1},{8,2},{24,3},{1,8},{17,9},{9,10},{25,11},{2,16},{18,1... | collective-permute-start | bytes 3440648 | tf_op jit(solution)/shard_map/ppermute | solution.py:958
  738.2 74.0 %reduce-scatter.10.cloned.1.call-done = bf16[320,1792]{1,0:T(8,128)(2,1)} async-done(((bf16[2560,1792]{1,0:T(8,128)(2,1)}), bf16[320,1792]{1,0:T(8,128)(2,1)}) %reduce-scatter.10.cloned.1.call-update) | async-done | bytes 1146896 | tf_op jit(solution)/shard_map/reduce_scatter | solution.py:955
  (376 shorter events, 361.3 us)
Async XLA Ops:
  7.2 192.1 %all-gather.6.cloned.1.call-start = ((), (), s32[]{:S(2)}) async-start(), calls=%async_computation.5 | async-start | bytes 5898240 | tf_op jit(solution)/shard_map/all_gather | solution.py:844
  11.4 226.4 %all-gather.8.cloned.1.call-start = ((), (), s32[]{:S(2)}) async-start(), calls=%async_computation.6 | async-start | bytes 3686400 | tf_op jit(solution)/shard_map/all_gather | solution.py:845
  13.1 326.6 %all-gather.12.cloned.1.call-start = ((), (), s32[]{:S(2)}) async-start(), calls=%async_computation.8 | async-start | bytes 10321920 | tf_op jit(solution)/shard_map/all_gather | solution.py:847
  13.8 337.0 %all-gather.10.cloned.1.call-start = ((), (), s32[]{:S(2)}) async-start(), calls=%async_computation.7 | async-start | bytes 10321920 | tf_op jit(solution)/shard_map/all_gather | solution.py:846
  14.4 347.5 %all-gather.14.cloned.1.call-start = ((), (), s32[]{:S(2)}) async-start(), calls=%async_computation.9 | async-start | bytes 10321920 | tf_op jit(solution)/shard_map/all_gather | solution.py:848
  14.6 33.0 %collective-permute-start.6 = (bf16[1,288]{1,0:T(2,128)(2,1)S(1)}, bf16[1,288]{1,0:T(2,128)(2,1)S(1)}, u32[]{:S(2)}, u32[]{:S(2)}) collective-permute-start(bf16[1,288]{1,0:T(2,128)(2,1)S(1)} %broadcast_in_dim.10), channel_id=1, source_target_pairs={{0,1},{1,0},{2,3},{3,2},{4,5},{5,4},{6,7},{7,6},{8,9},{9,8},{10,11... | collective-permute-start | bytes 1736 | tf_op jit(solution)/shard_map/ppermute | solution.py:599
  30.4 57.8 %collective-permute-start.35 = (bf16[64,2560]{1,0:T(8,128)(2,1)}, bf16[64,2560]{1,0:T(8,128)(2,1)}, u32[]{:S(2)}, u32[]{:S(2)}) collective-permute-start(bf16[64,2560]{1,0:T(8,128)(2,1)} %get-tuple-element.130), channel_id=1, source_target_pairs={{0,3},{1,0},{2,1},{3,2},{4,7},{5,4},{6,5},{7,6},{8,11},{9,8},{10,9... | collective-permute-start | bytes 983048 | tf_op jit(solution)/shard_map/ppermute | solution.py:632
  40.1 51.3 %collective-permute-start.32 = (bf16[64,2560]{1,0:T(8,128)(2,1)S(1)}, bf16[64,2560]{1,0:T(8,128)(2,1)}, u32[]{:S(2)}, u32[]{:S(2)}) collective-permute-start(bf16[64,2560]{1,0:T(8,128)(2,1)S(1)} %get-tuple-element.131), channel_id=1, source_target_pairs={{0,1},{1,2},{2,3},{3,0},{4,5},{5,6},{6,7},{7,4},{8,9},{9,10},{10,1... | collective-permute-start | bytes 983048 | tf_op jit(solution)/shard_map/ppermute | solution.py:632
  40.9 50.5 %collective-permute-start.3 = (bf16[64,2560]{1,0:T(8,128)(2,1)}, bf16[64,2560]{1,0:T(8,128)(2,1)}, u32[]{:S(2)}, u32[]{:S(2)}) collective-permute-start(bf16[64,2560]{1,0:T(8,128)(2,1)} %get-tuple-element.134), channel_id=1, source_target_pairs={{0,3},{1,0},{2,1},{3,2},{4,7},{5,4},{6,5},{7,6},{8,11},{9,8},{10,9... | collective-permute-start | bytes 983048 | tf_op jit(solution)/shard_map/ppermute | solution.py:632
  44.7 50.5 %collective-permute-start = (bf16[64,2560]{1,0:T(8,128)(2,1)S(1)}, bf16[64,2560]{1,0:T(8,128)(2,1)}, u32[]{:S(2)}, u32[]{:S(2)}) collective-permute-start(bf16[64,2560]{1,0:T(8,128)(2,1)S(1)} %get-tuple-element.135), channel_id=1, source_target_pairs={{0,1},{1,2},{2,3},{3,0},{4,5},{5,6},{6,7},{7,4},{8,9},{9,10},{10,1... | collective-permute-start | bytes 983048 | tf_op jit(solution)/shard_map/ppermute | solution.py:632
  47.7 20.1 %collective-permute-start.7 = (bf16[2,288]{1,0:T(2,128)(2,1)S(1)}, bf16[2,288]{1,0:T(2,128)(2,1)S(1)}, u32[]{:S(2)}, u32[]{:S(2)}) collective-permute-start(bf16[2,288]{1,0:T(2,128)(2,1)S(1)} %pad_maximum_fusion.14), channel_id=1, source_target_pairs={{0,2},{1,3},{2,0},{3,1},{4,6},{5,7},{6,4},{7,5},{8,10},{9,11},{10,... | collective-permute-start | bytes 3464 | tf_op jit(solution)/shard_map/ppermute | solution.py:599
  86.1 112.2 %collective-permute-start.25 = (bf16[896,640]{1,0:T(8,128)(2,1)}, bf16[896,640]{1,0:T(8,128)(2,1)S(1)}, u32[]{:S(2)}, u32[]{:S(2)}) collective-permute-start(bf16[896,640]{1,0:T(8,128)(2,1)} %param.22), channel_id=1, source_target_pairs={{0,0},{1,16},{2,8},{3,24},{8,1},{9,17},{10,9},{11,25},{16,2},{17,1... | collective-permute-start | bytes 3440648 | tf_op jit(solution)/shard_map/ppermute | solution.py:843
  88.3 62.2 %collective-permute-start.36 = (bf16[64,2560]{1,0:T(8,128)(2,1)}, bf16[64,2560]{1,0:T(8,128)(2,1)}, u32[]{:S(2)}, u32[]{:S(2)}) collective-permute-start(bf16[64,2560]{1,0:T(8,128)(2,1)} %collective-permute-done.35), channel_id=1, source_target_pairs={{0,3},{1,0},{2,1},{3,2},{4,7},{5,4},{6,5},{7,6},{8,11},{9,8},{10,9... | collective-permute-start | bytes 983048 | tf_op jit(solution)/shard_map/ppermute | solution.py:632
  91.4 59.1 %collective-permute-start.33 = (bf16[64,2560]{1,0:T(8,128)(2,1)}, bf16[64,2560]{1,0:T(8,128)(2,1)S(1)}, u32[]{:S(2)}, u32[]{:S(2)}) collective-permute-start(bf16[64,2560]{1,0:T(8,128)(2,1)} %collective-permute-done.32), channel_id=1, source_target_pairs={{0,1},{1,2},{2,3},{3,0},{4,5},{5,6},{6,7},{7,4},{8,9},{9,10},{10,1... | collective-permute-start | bytes 983048 | tf_op jit(solution)/shard_map/ppermute | solution.py:632
  91.4 70.9 %collective-permute-start.4 = (bf16[64,2560]{1,0:T(8,128)(2,1)}, bf16[64,2560]{1,0:T(8,128)(2,1)S(1)}, u32[]{:S(2)}, u32[]{:S(2)}) collective-permute-start(bf16[64,2560]{1,0:T(8,128)(2,1)} %collective-permute-done.3), channel_id=1, source_target_pairs={{0,3},{1,0},{2,1},{3,2},{4,7},{5,4},{6,5},{7,6},{8,11},{9,8},{10,9... | collective-permute-start | bytes 983048 | tf_op jit(solution)/shard_map/ppermute | solution.py:632
  95.2 67.6 %collective-permute-start.1 = (bf16[64,2560]{1,0:T(8,128)(2,1)}, bf16[64,2560]{1,0:T(8,128)(2,1)S(1)}, u32[]{:S(2)}, u32[]{:S(2)}) collective-permute-start(bf16[64,2560]{1,0:T(8,128)(2,1)} %collective-permute-done), channel_id=1, source_target_pairs={{0,1},{1,2},{2,3},{3,0},{4,5},{5,6},{6,7},{7,4},{8,9},{9,10},{10,1... | collective-permute-start | bytes 983048 | tf_op jit(solution)/shard_map/ppermute | solution.py:632
  150.5 135.4 %collective-permute-start.37 = (bf16[64,2560]{1,0:T(8,128)(2,1)}, bf16[64,2560]{1,0:T(8,128)(2,1)}, u32[]{:S(2)}, u32[]{:S(2)}) collective-permute-start(bf16[64,2560]{1,0:T(8,128)(2,1)} %collective-permute-done.36), channel_id=1, source_target_pairs={{0,3},{1,0},{2,1},{3,2},{4,7},{5,4},{6,5},{7,6},{8,11},{9,8},{10,9... | collective-permute-start | bytes 983048 | tf_op jit(solution)/shard_map/ppermute | solution.py:632
  150.5 47.0 %collective-permute-start.34 = (bf16[64,2560]{1,0:T(8,128)(2,1)S(1)}, bf16[64,2560]{1,0:T(8,128)(2,1)S(1)}, u32[]{:S(2)}, u32[]{:S(2)}) collective-permute-start(bf16[64,2560]{1,0:T(8,128)(2,1)S(1)} %collective-permute-done.33), channel_id=1, source_target_pairs={{0,1},{1,2},{2,3},{3,0},{4,5},{5,6},{6,7},{7,4},{8,9},{9,10},{10,1... | collective-permute-start | bytes 983048 | tf_op jit(solution)/shard_map/ppermute | solution.py:632
  162.3 31.6 %collective-permute-start.5 = (bf16[64,2560]{1,0:T(8,128)(2,1)S(1)}, bf16[64,2560]{1,0:T(8,128)(2,1)S(1)}, u32[]{:S(2)}, u32[]{:S(2)}) collective-permute-start(bf16[64,2560]{1,0:T(8,128)(2,1)S(1)} %collective-permute-done.4), channel_id=1, source_target_pairs={{0,3},{1,0},{2,1},{3,2},{4,7},{5,4},{6,5},{7,6},{8,11},{9,8},{10,9... | collective-permute-start | bytes 983048 | tf_op jit(solution)/shard_map/ppermute | solution.py:632
  162.8 27.1 %collective-permute-start.2 = (bf16[64,2560]{1,0:T(8,128)(2,1)S(1)}, bf16[64,2560]{1,0:T(8,128)(2,1)S(1)}, u32[]{:S(2)}, u32[]{:S(2)}) collective-permute-start(bf16[64,2560]{1,0:T(8,128)(2,1)S(1)} %collective-permute-done.1), channel_id=1, source_target_pairs={{0,1},{1,2},{2,3},{3,0},{4,5},{5,6},{6,7},{7,4},{8,9},{9,10},{10,1... | collective-permute-start | bytes 983048 | tf_op jit(solution)/shard_map/ppermute | solution.py:632
  199.3 515.6 %reduce-scatter.14.cloned.1.call-start = ((), (), s32[]{:S(2)}) async-start(), calls=%async_computation.14 | async-start | bytes 10321920 | tf_op jit(solution)/shard_map/reduce_scatter | solution.py:955
  245.7 17.5 %collective-permute-start.16 = (bf16[64,2560]{1,0:T(8,128)(2,1)S(1)}, bf16[64,2560]{1,0:T(8,128)(2,1)S(1)}, u32[]{:S(2)}, u32[]{:S(2)}) collective-permute-start(bf16[64,2560]{1,0:T(8,128)(2,1)S(1)} %get-tuple-element.120), channel_id=1, source_target_pairs={{0,3},{1,0},{2,1},{3,2},{4,7},{5,4},{6,5},{7,6},{8,11},{9,8},{10,9... | collective-permute-start | bytes 983048 | tf_op jit(solution)/shard_map/ppermute | solution.py:646
  320.9 18.1 %collective-permute-start.24 = (bf16[64,2560]{1,0:T(8,128)(2,1)S(1)}, bf16[64,2560]{1,0:T(8,128)(2,1)S(1)}, u32[]{:S(2)}, u32[]{:S(2)}) collective-permute-start(bf16[64,2560]{1,0:T(8,128)(2,1)S(1)} %collective-permute-done.23), channel_id=1, source_target_pairs={{0,3},{1,0},{2,1},{3,2},{4,7},{5,4},{6,5},{7,6},{8,11},{9,8},{10,9... | collective-permute-start | bytes 983048 | tf_op jit(solution)/shard_map/ppermute | solution.py:632
  394.1 331.0 %reduce-scatter.8.cloned.1.call-start = ((), (), s32[]{:S(2)}) async-start(), calls=%async_computation.11 | async-start | bytes 3686400 | tf_op jit(solution)/shard_map/reduce_scatter | solution.py:955
  470.4 17.4 %collective-permute-start.44 = (bf16[64,2560]{1,0:T(8,128)(2,1)S(1)}, bf16[64,2560]{1,0:T(8,128)(2,1)S(1)}, u32[]{:S(2)}, u32[]{:S(2)}) collective-permute-start(bf16[64,2560]{1,0:T(8,128)(2,1)S(1)} %get-tuple-element.129), channel_id=1, source_target_pairs={{0,1},{1,2},{2,3},{3,0},{4,5},{5,6},{6,7},{7,4},{8,9},{9,10},{10,1... | collective-permute-start | bytes 983048 | tf_op jit(solution)/shard_map/ppermute | solution.py:632
  492.6 21.6 %collective-permute-start.49 = (bf16[64,2560]{1,0:T(8,128)(2,1)S(1)}, bf16[64,2560]{1,0:T(8,128)(2,1)S(1)}, u32[]{:S(2)}, u32[]{:S(2)}) collective-permute-start(bf16[64,2560]{1,0:T(8,128)(2,1)S(1)} %collective-permute-done.48), channel_id=1, source_target_pairs={{0,3},{1,0},{2,1},{3,2},{4,7},{5,4},{6,5},{7,6},{8,11},{9,8},{10,9... | collective-permute-start | bytes 983048 | tf_op jit(solution)/shard_map/ppermute | solution.py:632
  525.9 205.6 %reduce-scatter.6.cloned.1.call-start = ((), (), s32[]{:S(2)}) async-start(), calls=%async_computation.10 | async-start | bytes 5898240 | tf_op jit(solution)/shard_map/reduce_scatter | solution.py:955
  579.4 155.9 %reduce-scatter.12.cloned.1.call-start = ((), (), s32[]{:S(2)}) async-start(), calls=%async_computation.13 | async-start | bytes 10321920 | tf_op jit(solution)/shard_map/reduce_scatter | solution.py:955
  590.6 221.6 %reduce-scatter.10.cloned.1.call-start = ((), (), s32[]{:S(2)}) async-start(), calls=%async_computation.12 | async-start | bytes 10321920 | tf_op jit(solution)/shard_map/reduce_scatter | solution.py:955
  643.4 16.8 %collective-permute-start.28 = (bf16[64,2560]{1,0:T(8,128)(2,1)S(1)}, bf16[64,2560]{1,0:T(8,128)(2,1)S(1)}, u32[]{:S(2)}, u32[]{:S(2)}) collective-permute-start(bf16[64,2560]{1,0:T(8,128)(2,1)S(1)} %get-tuple-element.107), channel_id=1, source_target_pairs={{0,1},{1,2},{2,3},{3,0},{4,5},{5,6},{6,7},{7,4},{8,9},{9,10},{10,1... | collective-permute-start | bytes 983048 | tf_op jit(solution)/shard_map/ppermute | solution.py:646
  644.0 16.2 %collective-permute-start.30 = (bf16[64,2560]{1,0:T(8,128)(2,1)S(1)}, bf16[64,2560]{1,0:T(8,128)(2,1)S(1)}, u32[]{:S(2)}, u32[]{:S(2)}) collective-permute-start(bf16[64,2560]{1,0:T(8,128)(2,1)S(1)} %get-tuple-element.108), channel_id=1, source_target_pairs={{0,3},{1,0},{2,1},{3,2},{4,7},{5,4},{6,5},{7,6},{8,11},{9,8},{10,9... | collective-permute-start | bytes 983048 | tf_op jit(solution)/shard_map/ppermute | solution.py:646
  714.9 100.1 %collective-permute-start.63 = (bf16[896,640]{1,0:T(8,128)(2,1)}, bf16[896,640]{1,0:T(8,128)(2,1)}, u32[]{:S(2)}, u32[]{:S(2)}) collective-permute-start(bf16[896,640]{1,0:T(8,128)(2,1)} %reduce-scatter.14.cloned.1.call-done), channel_id=1, source_target_pairs={{0,0},{16,1},{8,2},{24,3},{1,8},{17,9},{9,10},{25,11},{2,16},{18,1... | collective-permute-start | bytes 3440648 | tf_op jit(solution)/shard_map/ppermute | solution.py:958
  (73 other events, 833.2 us)
Sparse Core Ops, SparseCore 0:
  11.5 46.4 all-gather.5
  59.9 32.7 all-gather.7
  94.6 67.9 all-gather.11
  164.3 61.7 all-gather.9
  228.4 62.9 all-gather.13
  394.3 82.6 reduce-scatter.13
  526.0 61.5 reduce-scatter.7
  591.0 56.5 reduce-scatter.5
  651.2 75.3 reduce-scatter.11
  730.1 82.0 reduce-scatter.9
